TPU v7x, 32 devices: a whole 2x2x4 slice. The times are simulated.
32 devices in a mesh: dp: 8 (over z, x), th: 2 (over core), tw: 2 (over y).
Axes of the slice: x: 2, y: 2, z: 4, core: 2. Of those that a mesh axis runs over, the one named last changes fastest.
Arguments:
- tokens: bfloat16 [16, 1536, 768], P('dp', ('th', 'tw')), may hold values from -6 to 6
- segment_ids: int32 [16, 1536], P('dp'), may hold values from 0 to 7, never falling along the last dimension, each value on 1 to 768 neighbouring positions
- norm1_gain: float32 [768], replicated, may hold values from 0.5 to 1.5
- norm1_shift: float32 [768], replicated, may hold values from -3 to 3
- w_qkv: bfloat16 [3, 768, 768], P(None, None, ('th', 'tw')), may hold values from -0.21875 to 0.21875
- b_qv: float32 [2, 768], P(None, ('th', 'tw')), may hold values from -3 to 3
- w_out: bfloat16 [768, 768], P(('th', 'tw')), may hold values from -0.875 to 0.875
- b_out: float32 [768], replicated, may hold values from -3 to 3
- norm2_gain: float32 [768], replicated, may hold values from 0.5 to 1.5
- norm2_shift: float32 [768], replicated, may hold values from -3 to 3
- w_up: bfloat16 [768, 3072], replicated, may hold values from -0.21875 to 0.21875
- b_up: float32 [3072], replicated, may hold values from -3 to 3
- w_down: bfloat16 [3072, 768], replicated, may hold values from -0.109375 to 0.109375
- b_down: float32 [768], replicated, may hold values from -3 to 3
- cotangent: bfloat16 [16, 1536, 768], P('dp', ('th', 'tw')), may hold values from -6 to 6
Outputs:
- block_out: bfloat16 [16, 1536, 768], P('dp', ('th', 'tw'))
- grad_tokens: bfloat16 [16, 1536, 768], P('dp', ('th', 'tw'))
- grad_norm1_gain: float32 [768], replicated
- grad_norm1_shift: float32 [768], replicated
- grad_w_qkv: float32 [3, 768, 768], P(None, None, ('th', 'tw'))
- grad_b_qv: float32 [2, 768], P(None, ('th', 'tw'))
- grad_w_out: float32 [768, 768], P(('th', 'tw'))
- grad_b_out: float32 [768], replicated
- grad_norm2_gain: float32 [768], replicated
- grad_norm2_shift: float32 [768], replicated
- grad_w_up: float32 [768, 3072], replicated
- grad_b_up: float32 [3072], replicated
- grad_w_down: float32 [3072, 768], replicated
- grad_b_down: float32 [768], replicated
Inputs may be any that keep to these rules, and one draw needn't show every extreme that they name: `segment_ids`: within each row the ids never fall, and one image holds 1 to 768 tokens.
All inputs are finite; a program needn't handle non-finite values.
Results may differ from a plain program's by a relative error of at most 0.015.
Values may be sent and summed in bfloat16 or wider, within the bound.
A program may use at most 192 MiB of HBM per device.

v0:
```python
import jax
import jax.numpy as jnp
from jax import lax
from jax.sharding import PartitionSpec as P

HD = 64


EPSILON = 1e-06


def layer_norm(field, norm_gain, norm_shift):
    average = jnp.mean(field, axis=-1, keepdims=True)
    centred = field - average
    spread = jnp.mean(centred * centred, axis=-1, keepdims=True)
    return centred * lax.rsqrt(spread + EPSILON) * norm_gain + norm_shift


def gelu_exact(field):
    return jax.nn.gelu(field, approximate=False)


def masked_scores(query_block, key_rows, row_seg, offset, block_rows):
    score_scale = query_block.shape[-1] ** (-0.5)
    same_image = row_seg[offset : offset + block_rows, None] == row_seg[None, :]
    scores = (
        jnp.einsum("qhe,khe->hqk", query_block, key_rows, preferred_element_type=jnp.float32)
        * score_scale
    )
    return jnp.where(same_image[None], scores, -1000000000.0)


def row_forward(row_items):
    row_qkv, row_seg = row_items
    length = row_qkv.shape[1]
    head_count = row_qkv.shape[2] // HD
    key_rows = row_qkv[1].reshape(length, head_count, HD)
    value_rows = row_qkv[2].reshape(length, head_count, HD)
    block_rows = min(512, length)
    head_outs = []
    log_totals = []
    for offset in range(0, length, block_rows):
        query_block = row_qkv[0, offset : offset + block_rows].reshape(block_rows, head_count, HD)
        scores = masked_scores(query_block, key_rows, row_seg, offset, block_rows)
        row_peak = jnp.max(scores, axis=-1, keepdims=True)
        exponent = jnp.exp(scores - row_peak)
        denominator = jnp.sum(exponent, axis=-1, keepdims=True)
        weights_low = (exponent / denominator).astype(jnp.bfloat16)
        head_out = jnp.einsum(
            "hqk,khe->qhe", weights_low, value_rows, preferred_element_type=jnp.float32
        )
        head_outs.append(head_out.reshape(block_rows, head_count * HD).astype(jnp.bfloat16))
        log_totals.append((row_peak + jnp.log(denominator))[..., 0])
    return (jnp.concatenate(head_outs, 0), jnp.concatenate(log_totals, 1))


def row_backward(row_items):
    row_qkv, row_grad, row_total, row_seg = row_items
    length = row_qkv.shape[1]
    head_count = row_qkv.shape[2] // HD
    score_scale = HD ** (-0.5)
    key_rows = row_qkv[1].reshape(length, head_count, HD)
    value_rows = row_qkv[2].reshape(length, head_count, HD)
    block_rows = min(512, length)
    key_grad = jnp.zeros((length, head_count, HD), jnp.float32)
    value_grad = jnp.zeros((length, head_count, HD), jnp.float32)
    query_grads = []
    for offset in range(0, length, block_rows):
        query_block = row_qkv[0, offset : offset + block_rows].reshape(block_rows, head_count, HD)
        upstream = row_grad[offset : offset + block_rows].reshape(block_rows, head_count, HD)
        scores = masked_scores(query_block, key_rows, row_seg, offset, block_rows)
        probability = jnp.exp(scores - row_total[:, offset : offset + block_rows, None])
        value_grad = value_grad + jnp.einsum(
            "hqk,qhe->khe",
            probability.astype(jnp.bfloat16),
            upstream,
            preferred_element_type=jnp.float32,
        )
        prob_grad = jnp.einsum(
            "qhe,khe->hqk", upstream, value_rows, preferred_element_type=jnp.float32
        )
        row_inner = jnp.sum(probability * prob_grad, axis=-1, keepdims=True)
        score_grad = (probability * (prob_grad - row_inner)).astype(jnp.bfloat16) * score_scale
        query_grad = jnp.einsum(
            "hqk,khe->qhe", score_grad, key_rows, preferred_element_type=jnp.float32
        )
        query_grads.append(query_grad.reshape(block_rows, head_count * HD))
        key_grad = key_grad + jnp.einsum(
            "hqk,qhe->khe", score_grad, query_block, preferred_element_type=jnp.float32
        )
    stacked = jnp.stack(
        [
            jnp.concatenate(query_grads, 0),
            key_grad.reshape(length, head_count * HD),
            value_grad.reshape(length, head_count * HD),
        ]
    )
    return stacked.astype(jnp.bfloat16)


def body(
    tokens,
    segment_ids,
    norm1_gain,
    norm1_shift,
    w_qkv,
    b_qv,
    w_out,
    b_out,
    norm2_gain,
    norm2_shift,
    w_up,
    b_up,
    w_down,
    b_down,
    cotangent,
):
    inputs = tokens.astype(jnp.float32)
    normed_one, norm_one_back = jax.vjp(layer_norm, inputs, norm1_gain, norm1_shift)
    normed_low = normed_one.astype(jnp.bfloat16)
    gathered = lax.all_gather(normed_low, ("th", "tw"), axis=1, tiled=True)
    bias_rows = jnp.stack([b_qv[0], jnp.zeros_like(b_qv[0]), b_qv[1]])
    projected = jnp.einsum("rld,cde->rcle", gathered, w_qkv, preferred_element_type=jnp.float32)
    projected_low = (projected + bias_rows[None, :, None, :]).astype(jnp.bfloat16)
    heads_out, totals = lax.map(row_forward, (projected_low, segment_ids))
    partial_out = jnp.einsum("rle,ed->rld", heads_out, w_out, preferred_element_type=jnp.float32)
    branch = (
        lax.psum_scatter(
            partial_out.astype(jnp.bfloat16), ("th", "tw"), scatter_dimension=1, tiled=True
        ).astype(jnp.float32)
        + b_out
    )
    middle = inputs + branch
    normed_two, norm_two_back = jax.vjp(layer_norm, middle, norm2_gain, norm2_shift)
    second_low = normed_two.astype(jnp.bfloat16)
    hidden_pre = (
        jnp.einsum("rld,df->rlf", second_low, w_up, preferred_element_type=jnp.float32) + b_up
    )
    activated, gelu_back = jax.vjp(gelu_exact, hidden_pre)
    active_low = activated.astype(jnp.bfloat16)
    block_out = middle + (
        jnp.einsum("rlf,fd->rld", active_low, w_down, preferred_element_type=jnp.float32) + b_down
    )
    upstream = cotangent.astype(jnp.float32)
    grad_w_down = jnp.einsum(
        "rlf,rld->fd", active_low, cotangent, preferred_element_type=jnp.float32
    )
    grad_b_down = jnp.sum(upstream, axis=(0, 1))
    grad_active = jnp.einsum("rld,fd->rlf", cotangent, w_down, preferred_element_type=jnp.float32)
    grad_hidden = gelu_back(grad_active)[0].astype(jnp.bfloat16)
    grad_w_up = jnp.einsum(
        "rld,rlf->df", second_low, grad_hidden, preferred_element_type=jnp.float32
    )
    grad_b_up = jnp.sum(grad_hidden.astype(jnp.float32), axis=(0, 1))
    grad_normed_two = jnp.einsum(
        "rlf,df->rld", grad_hidden, w_up, preferred_element_type=jnp.float32
    )
    grad_mid_norm, grad_gain_two, grad_shift_two = norm_two_back(grad_normed_two)
    grad_middle = upstream + grad_mid_norm
    grad_branch = grad_middle.astype(jnp.bfloat16)
    grad_b_out = jnp.sum(grad_branch.astype(jnp.float32), axis=(0, 1))
    grad_whole = lax.all_gather(grad_branch, ("th", "tw"), axis=1, tiled=True)
    grad_heads = jnp.einsum(
        "rld,ed->rle", grad_whole, w_out, preferred_element_type=jnp.float32
    ).astype(jnp.bfloat16)
    grad_w_out = jnp.einsum(
        "rle,rld->ed", heads_out, grad_whole, preferred_element_type=jnp.float32
    )
    grad_qkv = lax.map(row_backward, (projected_low, grad_heads, totals, segment_ids))
    grad_w_qkv = jnp.einsum("rld,rcle->cde", gathered, grad_qkv, preferred_element_type=jnp.float32)
    grad_b_qv = jnp.sum(grad_qkv[:, 0::2].astype(jnp.float32), axis=(0, 2))
    grad_normed = jnp.einsum("rcle,cde->rld", grad_qkv, w_qkv, preferred_element_type=jnp.float32)
    grad_tile = lax.psum_scatter(
        grad_normed.astype(jnp.bfloat16), ("th", "tw"), scatter_dimension=1, tiled=True
    ).astype(jnp.float32)
    grad_inputs, grad_gain_one, grad_shift_one = norm_one_back(grad_tile)
    grad_tokens = (grad_middle + grad_inputs).astype(jnp.bfloat16)
    head_sums = (
        lax.psum(grad_w_qkv.astype(jnp.bfloat16), "dp").astype(jnp.float32),
        lax.psum(grad_b_qv.astype(jnp.bfloat16), "dp").astype(jnp.float32),
        lax.psum(grad_w_out.astype(jnp.bfloat16), "dp").astype(jnp.float32),
    )
    shared = lax.psum(
        (
            grad_gain_one,
            grad_shift_one,
            grad_b_out,
            grad_gain_two,
            grad_shift_two,
            grad_w_up,
            grad_b_up,
            grad_w_down,
            grad_b_down,
        ),
        ("dp", "th", "tw"),
    )
    return (
        block_out.astype(jnp.bfloat16),
        grad_tokens,
        shared[0],
        shared[1],
        head_sums[0],
        head_sums[1],
        head_sums[2],
        shared[2],
        shared[3],
        shared[4],
        shared[5],
        shared[6],
        shared[7],
        shared[8],
    )


def solution(mesh):
    return jax.shard_map(
        body,
        mesh=mesh,
        in_specs=(
            P("dp", ("th", "tw"), None),
            P("dp", None),
            P(),
            P(),
            P(None, None, ("th", "tw")),
            P(None, ("th", "tw")),
            P(("th", "tw"), None),
            P(),
            P(),
            P(),
            P(),
            P(),
            P(),
            P(),
            P("dp", ("th", "tw"), None),
        ),
        out_specs=(
            P("dp", ("th", "tw"), None),
            P("dp", ("th", "tw"), None),
            P(),
            P(),
            P(None, None, ("th", "tw")),
            P(None, ("th", "tw")),
            P(("th", "tw"), None),
            P(),
            P(),
            P(),
            P(),
            P(),
            P(),
            P(),
        ),
        check_vma=False,
    )
```

profile of v0, /device:TPU:0, one launch (start us, length us, event | category | flops | bytes accessed | tf_op | source)
XLA Modules:
  0.0 1006.1 jit_solution(13144696597506998621)
XLA Ops:
  14.8 40.1 %all-gather.3.cloned.1.call-done = bf16[2,1536,768]{2,1,0:T(8,128)(2,1)} async-done(((bf16[2,384,768]{2,1,0:T(8,128)(2,1)}), bf16[2,1536,768]{2,1,0:T(8,128)(2,1)}) %all-gather.3.cloned.1.call-update) | async-done | bytes 4718608 | tf_op jit(solution)/shard_map/all_gather | solution.py:121
  61.6 59.1 %while.22 = (s32[]{:T(128)}, bf16[2,1536,192]{1,2,0:T(8,128)(2,1)S(1)}, f32[2,3,1536]{2,1,0:T(4,128)S(1)}, bf16[2,3,1536,192]{2,3,1,0:T(8,128)(2,1)}, s32[2,1536...) while((s32[]{:T(128)}, bf16[2,1536,192]{1,2,0:T(8,128)(2,1)S(1)}, ...), condition=%wide.region_9.10_spmd, body=%wide.region_2.9_spmd.sunk | while | flops 1901302272 | bytes 107581632 | solution.py:125
  125.8 47.9 %reduce-scatter.3.cloned.1.call-done = bf16[2,384,768]{2,1,0:T(8,128)(2,1)} async-done(((bf16[2,1536,768]{2,1,0:T(8,128)(2,1)}), bf16[2,384,768]{2,1,0:T(8,128)(2,1)}) %reduce-scatter.3.cloned.1.call-update) | async-done | bytes 1179664 | tf_op jit(solution)/shard_map/reduce_scatter | solution.py:128
  186.7 23.6 %multiply_convert_fusion.3 = (bf16[2,384,3072]{2,1,0:T(8,128)(2,1)}, f32[2,384,3072]{2,1,0:T(8,128)}) fusion(f32[2,384,3072]{2,1,0:T(8,128)S(1)} %get-tuple-element.164, f32[3072]{0:T(1024)S(1)} %copy-done.45, u8[384,3072]{1,0:T(8,128)(4,1)S(1)} %get-tuple-element.78, u8[384,3072]{1,0:T(8,128)(4,1)S(1)} %get-tuple-element.77), kind=kLoop, calls=%fused_computation.126 | loop fusion | flops 167510016 | bytes 25964544 | tf_op jit(solution)/shard_map/convert_element_type | solution.py:140
  210.4 12.5 %convert_reduce_fusion = (f32[3072]{0:T(1024)}, bf16[2,384,3072]{2,1,0:T(8,128)(2,1)}) fusion(f32[2,384,3072]{2,1,0:T(8,128)} %get-tuple-element.123, bf16[2,384,768]{2,1,0:T(8,128)(2,1)S(1)} %copy-done.15, bf16[3072,768]{1,0:T(8,128)(2,1)} %param.31, f32[2,384,3072]{2,1,0:T(8,128)S(1)} %get-tuple-element.164, f32[3072]{0:T(1024)S(1)} %copy-done.45), kind=kOutput, calls=%fused_computation.124 | convolution fusion | flops 3663983616 | bytes 29515776 | tf_op jit(solution)/shard_map/rld,fd->rlf/dot_general | solution.py:149
  235.9 37.6 %all-gather.5.cloned.1.call-done = bf16[2,1536,768]{2,1,0:T(8,128)(2,1)} async-done(((bf16[2,384,768]{2,1,0:T(8,128)(2,1)}), bf16[2,1536,768]{2,1,0:T(8,128)(2,1)}) %all-gather.5.cloned.1.call-update) | async-done | bytes 4718608 | tf_op jit(solution)/shard_map/all_gather | solution.py:162
  278.5 254.2 %while.23 = (s32[]{:T(128)}, bf16[2,3,1536,192]{2,3,1,0:T(8,128)(2,1)}, bf16[2,3,1536,192]{2,3,1,0:T(8,128)(2,1)}, s32[2,1536]{1,0:T(2,128)S(1)}, f32[2,3,1536]{...) while((s32[]{:T(128)}, ...), condition=%wide.region_19.20_spmd, body=%wide.region_15.19_spmd.sunk | while | flops 4682926080 | bytes 364640672 | solution.py:169
  305.5 15.2 %fusion.377 = bf16[3,64,512]{2,1,0:T(8,128)(2,1)} fusion(bf16[1536,3,64]{0,2,1:T(8,128)(2,1)S(1)} %bitcast.312, f32[3,512,1536]{2,1,0:T(8,128)} %copy-done.4, f32[3,512,1536]{2,1,0:T(8,128)} %fusion.371), kind=kOutput, calls=%fused_computation.94.clone.1 | convolution fusion | flops 320965632 | bytes 19660800 | tf_op jit(solution)/shard_map/while/body/eval_jaxpr/hqk,khe->qhe/dot_general | solution.py:84
  320.6 15.3 %fusion.372 = f32[3,64,1536]{2,1,0:T(8,128)} fusion(bf16[512,3,64]{0,2,1:T(8,128)(2,1)} %bitcast.323, f32[3,512,1536]{2,1,0:T(8,128)} %copy-done.4, f32[3,512,1536]{2,1,0:T(8,128)} %fusion.371), kind=kOutput, calls=%fused_computation.63.clone.1 | convolution fusion | flops 320867328 | bytes 20250624 | tf_op jit(solution)/shard_map/while/body/eval_jaxpr/hqk,qhe->khe/dot_general | solution.py:88
  341.2 14.4 %fusion.379 = bf16[3,64,512]{2,1,0:T(8,128)(2,1)S(1)} fusion(bf16[1536,3,64]{0,2,1:T(8,128)(2,1)S(1)} %bitcast.313, f32[3,512,1536]{2,1,0:T(8,128)} %copy-done.3, f32[3,512,1536]{2,1,0:T(8,128)} %fusion.375), kind=kOutput, calls=%fused_computation.92.clone.1 | convolution fusion | flops 320965632 | bytes 19660800 | tf_op jit(solution)/shard_map/while/body/eval_jaxpr/hqk,khe->qhe/dot_general | solution.py:84
  360.7 15.0 %fusion.378 = bf16[3,64,512]{2,1,0:T(8,128)(2,1)} fusion(bf16[1536,3,64]{0,2,1:T(8,128)(2,1)S(1)} %bitcast.314, f32[3,512,1536]{2,1,0:T(8,128)} %copy-done.2, f32[3,512,1536]{2,1,0:T(8,128)} %fusion.373), kind=kOutput, calls=%fused_computation.93.clone.1 | convolution fusion | flops 320965632 | bytes 19660800 | tf_op jit(solution)/shard_map/while/body/eval_jaxpr/hqk,khe->qhe/dot_general | solution.py:84
  375.7 14.1 %fusion.374 = f32[3,64,1536]{2,1,0:T(8,128)} fusion(bf16[512,3,64]{0,2,1:T(8,128)(2,1)S(1)} %bitcast.321, f32[3,512,1536]{2,1,0:T(8,128)} %copy-done.2, f32[3,512,1536]{2,1,0:T(8,128)} %fusion.373), kind=kOutput, calls=%fused_computation.67.clone.1 | convolution fusion | flops 320867328 | bytes 20250624 | tf_op jit(solution)/shard_map/while/body/eval_jaxpr/hqk,qhe->khe/dot_general | solution.py:88
  389.8 14.1 %fusion.376 = bf16[3,64,1536]{2,1,0:T(8,128)(2,1)S(1)} fusion(f32[3,64,1536]{2,1,0:T(8,128)} %fusion.372, f32[3,64,1536]{2,1,0:T(8,128)} %fusion.374, bf16[512,3,64]{0,2,1:T(8,128)(2,1)S(1)} %bitcast.319, f32[3,512,1536]{2,1,0:T(8,128)} %copy-done.3, f32[3,512,1536]{2,1,0:T(8,128)} %fusion.375), kind=kOutput, calls=%fused_computation.79.clone.1 | convolution fusion | flops 321752064 | bytes 22020096 | tf_op jit(solution)/shard_map/while/body/eval_jaxpr/hqk,qhe->khe/dot_general | solution.py:88
  432.3 15.2 %fusion.377 = bf16[3,64,512]{2,1,0:T(8,128)(2,1)} fusion(bf16[1536,3,64]{0,2,1:T(8,128)(2,1)S(1)} %bitcast.312, f32[3,512,1536]{2,1,0:T(8,128)} %copy-done.4, f32[3,512,1536]{2,1,0:T(8,128)} %fusion.371), kind=kOutput, calls=%fused_computation.94.clone.1 | convolution fusion | flops 320965632 | bytes 19660800 | tf_op jit(solution)/shard_map/while/body/eval_jaxpr/hqk,khe->qhe/dot_general | solution.py:84
  447.5 15.3 %fusion.372 = f32[3,64,1536]{2,1,0:T(8,128)} fusion(bf16[512,3,64]{0,2,1:T(8,128)(2,1)} %bitcast.323, f32[3,512,1536]{2,1,0:T(8,128)} %copy-done.4, f32[3,512,1536]{2,1,0:T(8,128)} %fusion.371), kind=kOutput, calls=%fused_computation.63.clone.1 | convolution fusion | flops 320867328 | bytes 20250624 | tf_op jit(solution)/shard_map/while/body/eval_jaxpr/hqk,qhe->khe/dot_general | solution.py:88
  468.0 14.4 %fusion.379 = bf16[3,64,512]{2,1,0:T(8,128)(2,1)S(1)} fusion(bf16[1536,3,64]{0,2,1:T(8,128)(2,1)S(1)} %bitcast.313, f32[3,512,1536]{2,1,0:T(8,128)} %copy-done.3, f32[3,512,1536]{2,1,0:T(8,128)} %fusion.375), kind=kOutput, calls=%fused_computation.92.clone.1 | convolution fusion | flops 320965632 | bytes 19660800 | tf_op jit(solution)/shard_map/while/body/eval_jaxpr/hqk,khe->qhe/dot_general | solution.py:84
  487.5 15.0 %fusion.378 = bf16[3,64,512]{2,1,0:T(8,128)(2,1)} fusion(bf16[1536,3,64]{0,2,1:T(8,128)(2,1)S(1)} %bitcast.314, f32[3,512,1536]{2,1,0:T(8,128)} %copy-done.2, f32[3,512,1536]{2,1,0:T(8,128)} %fusion.373), kind=kOutput, calls=%fused_computation.93.clone.1 | convolution fusion | flops 320965632 | bytes 19660800 | tf_op jit(solution)/shard_map/while/body/eval_jaxpr/hqk,khe->qhe/dot_general | solution.py:84
  502.5 14.1 %fusion.374 = f32[3,64,1536]{2,1,0:T(8,128)} fusion(bf16[512,3,64]{0,2,1:T(8,128)(2,1)S(1)} %bitcast.321, f32[3,512,1536]{2,1,0:T(8,128)} %copy-done.2, f32[3,512,1536]{2,1,0:T(8,128)} %fusion.373), kind=kOutput, calls=%fused_computation.67.clone.1 | convolution fusion | flops 320867328 | bytes 20250624 | tf_op jit(solution)/shard_map/while/body/eval_jaxpr/hqk,qhe->khe/dot_general | solution.py:88
  516.6 14.1 %fusion.376 = bf16[3,64,1536]{2,1,0:T(8,128)(2,1)S(1)} fusion(f32[3,64,1536]{2,1,0:T(8,128)} %fusion.372, f32[3,64,1536]{2,1,0:T(8,128)} %fusion.374, bf16[512,3,64]{0,2,1:T(8,128)(2,1)S(1)} %bitcast.319, f32[3,512,1536]{2,1,0:T(8,128)} %copy-done.3, f32[3,512,1536]{2,1,0:T(8,128)} %fusion.375), kind=kOutput, calls=%fused_computation.79.clone.1 | convolution fusion | flops 321752064 | bytes 22020096 | tf_op jit(solution)/shard_map/while/body/eval_jaxpr/hqk,qhe->khe/dot_general | solution.py:88
  581.0 21.4 %psum.87 = bf16[2,192]{1,0:T(2,128)(2,1)S(1)} all-reduce(bf16[2,192]{1,0:T(2,128)(2,1)S(1)} %slice_reduce_fusion), channel_id=1, replica_groups=mesh['dp'=8,'th'=2,'tw'=2] {'dp'}, use_global_device_ids=true, to_apply=%region_29.30 | all-reduce | flops 384 | bytes 1536 | tf_op jit(solution)/shard_map/psum | solution.py:180
  603.0 20.9 %all-reduce.8.cloned.1.call-done = (bf16[3,768,192]{1,2,0:T(8,128)(2,1)}, bf16[192,768]{1,0:T(8,128)(2,1)}) async-done(((bf16[3,768,192]{1,2,0:T(8,128)(2,1)}, bf16[192,768]{1,0:T(8,128)(2,1)}), (bf16[3,768,192]{1,2,0:T(8,128)(2,1)}, bf16[192,768]{1,0:T(8,128)(2,1)})) %all-reduce.8.cloned.1.call-update) | async-done | bytes 1179664 | tf_op jit(solution)/shard_map/psum | solution.py:179
  628.2 45.2 %reduce-scatter.5.cloned.1.call-done = bf16[2,384,768]{2,1,0:T(8,128)(2,1)} async-done(((bf16[2,1536,768]{2,1,0:T(8,128)(2,1)}), bf16[2,384,768]{2,1,0:T(8,128)(2,1)}) %reduce-scatter.5.cloned.1.call-update) | async-done | bytes 1179664 | tf_op jit(solution)/shard_map/reduce_scatter | solution.py:173
  681.6 42.5 %all-reduce = (f32[768]{0:T(1024)}, f32[768]{0:T(1024)}, f32[768]{0:T(1024)}, f32[768]{0:T(1024)}, f32[768]{0:T(1024)}, /*index=5*/f32[3072]{0:T(1024)}, f32[768]{0:T(1024)}) all-reduce(f32[768]{0:T(1024)S(1)} %get-tuple-element.81, f32[768]{0:T(1024)S(1)} %get-tuple-element.85, ...), channel_id=1, replica_groups=mesh['dp'=8,'th'=2,'tw'=2] {'dp','th','tw'}, use_global_device_ids=true, to_apply=%region_24.25 | all-reduce | flops 7680 | bytes 61440 | tf_op jit(solution)/shard_map/psum | solution.py:183
  724.1 262.5 %all-reduce.6.cloned.1.call-done = (f32[768,3072]{1,0:T(8,128)}, f32[3072,768]{1,0:T(8,128)}) async-done(((f32[768,3072]{1,0:T(8,128)}, f32[3072,768]{1,0:T(8,128)}), (f32[768,3072]{1,0:T(8,128)}, f32[3072,768]{1,0:T(8,128)})) %all-reduce.6.cloned.1.call-update) | async-done | bytes 18874384 | tf_op jit(solution)/shard_map/psum | solution.py:183
  (252 shorter events, 258.8 us)
Async XLA Ops:
  7.2 47.7 %copy-start = (bf16[3,768,192]{1,2,0:T(8,128)(2,1)S(1)}, bf16[3,768,192]{1,2,0:T(8,128)(2,1)}, u32[]{:S(2)}) copy-start(bf16[3,768,192]{1,2,0:T(8,128)(2,1)} %param.23) | copy-start | bytes 2654212
  7.2 47.7 %all-gather.3.cloned.1.call-start = ((), (), s32[]{:S(2)}) async-start(), calls=%async_computation.2 | async-start | bytes 5898240 | tf_op jit(solution)/shard_map/all_gather | solution.py:121
  14.6 159.2 %reduce-scatter.3.cloned.1.call-start = ((), (), s32[]{:S(2)}) async-start(), calls=%async_computation.3 | async-start | bytes 5898240 | tf_op jit(solution)/shard_map/reduce_scatter | solution.py:128
  14.8 46.8 %copy-start.20 = (s32[2,1536]{1,0:T(2,128)S(1)}, s32[2,1536]{1,0:T(2,128)}, u32[]{:S(2)}) copy-start(s32[2,1536]{1,0:T(2,128)} %param.20) | copy-start | bytes 36868
  120.7 53.0 %copy-start.5 = (bf16[2,384,768]{2,1,0:T(8,128)(2,1)S(1)}, bf16[2,384,768]{2,1,0:T(8,128)(2,1)}, u32[]{:S(2)}) copy-start(bf16[2,384,768]{2,1,0:T(8,128)(2,1)} %param.19) | copy-start | bytes 3538948
  120.8 53.0 %copy-start.21 = (f32[768]{0:T(1024)S(1)}, f32[768]{0:T(1024)}, u32[]{:S(2)}) copy-start(f32[768]{0:T(1024)} %param.26) | copy-start | bytes 9220
  125.7 51.8 %copy-start.25 = (f32[768]{0:T(1024)S(1)}, f32[768]{0:T(1024)}, u32[]{:S(2)}) copy-start(f32[768]{0:T(1024)} %param.27) | copy-start | bytes 9220
  125.7 51.8 %copy-start.30 = (f32[768]{0:T(1024)S(1)}, f32[768]{0:T(1024)}, u32[]{:S(2)}) copy-start(f32[768]{0:T(1024)} %param.28) | copy-start | bytes 9220
  125.7 51.8 %copy-start.45 = (f32[3072]{0:T(1024)S(1)}, f32[3072]{0:T(1024)}, u32[]{:S(2)}) copy-start(f32[3072]{0:T(1024)} %param.30) | copy-start | bytes 36868
  125.7 147.7 %all-gather.5.cloned.1.call-start = ((), (), s32[]{:S(2)}) async-start(), calls=%async_computation.4 | async-start | bytes 5898240 | tf_op jit(solution)/shard_map/all_gather | solution.py:162
  175.6 57.5 %copy-start.23 = (f32[2,384]{1,0:T(2,128)}, f32[2,384]{1,0:T(2,128)S(1)}, u32[]{:S(2)}) copy-start(f32[2,384]{1,0:T(2,128)S(1)} %broadcast_multiply_fusion) | copy-start | bytes 9220
  177.5 55.5 %copy-start.27 = (f32[2,384]{1,0:T(2,128)}, f32[2,384]{1,0:T(2,128)S(1)}, u32[]{:S(2)}) copy-start(f32[2,384]{1,0:T(2,128)S(1)} %fusion.183) | copy-start | bytes 9220
  186.7 23.6 %copy-start.15 = (bf16[2,384,768]{2,1,0:T(8,128)(2,1)S(1)}, bf16[2,384,768]{2,1,0:T(8,128)(2,1)}, u32[]{:S(2)}) copy-start(bf16[2,384,768]{2,1,0:T(8,128)(2,1)} %param.33) | copy-start | bytes 3538948
  233.0 40.4 %copy-start.29 = (bf16[192,768]{1,0:T(8,128)(2,1)S(1)}, bf16[192,768]{1,0:T(8,128)(2,1)}, u32[]{:S(2)}) copy-start(bf16[192,768]{1,0:T(8,128)(2,1)} %param.25) | copy-start | bytes 884740
  233.0 45.4 %copy-start.39 = (f32[2,384]{1,0:T(2,128)}, f32[2,384]{1,0:T(2,128)S(1)}, u32[]{:S(2)}) copy-start(f32[2,384]{1,0:T(2,128)S(1)} %negate_multiply_fusion.2) | copy-start | bytes 9220
  235.8 388.1 %all-reduce.8.cloned.1.call-start = ((), (), s32[]{:S(2)}) async-start(), calls=%async_computation.7 | async-start | bytes 2359296 | tf_op jit(solution)/shard_map/psum | solution.py:179
  543.5 130.0 %reduce-scatter.5.cloned.1.call-start = ((), (), s32[]{:S(2)}) async-start(), calls=%async_computation.5 | async-start | bytes 5898240 | tf_op jit(solution)/shard_map/reduce_scatter | solution.py:173
  551.2 435.4 %all-reduce.6.cloned.1.call-start = ((), (), s32[]{:S(2)}) async-start(), calls=%async_computation.6 | async-start | bytes 37748736 | tf_op jit(solution)/shard_map/psum | solution.py:183
  580.6 92.9 %copy-start.33 = (f32[2,384]{1,0:T(2,128)S(1)}, f32[2,384]{1,0:T(2,128)}, u32[]{:S(2)}) copy-start(f32[2,384]{1,0:T(2,128)} %copy-done.32) | copy-start | bytes 9220
  580.6 92.9 %copy-start.34 = (f32[768]{0:T(1024)S(1)}, f32[768]{0:T(1024)}, u32[]{:S(2)}) copy-start(f32[768]{0:T(1024)} %param.21) | copy-start | bytes 9220
  580.6 95.2 %copy-start.42 = (f32[2,384]{1,0:T(2,128)S(1)}, f32[2,384]{1,0:T(2,128)}, u32[]{:S(2)}) copy-start(f32[2,384]{1,0:T(2,128)} %copy-done.41) | copy-start | bytes 9220
  580.6 95.2 %copy-start.38 = (f32[2,384]{1,0:T(2,128)S(1)}, f32[2,384]{1,0:T(2,128)}, u32[]{:S(2)}) copy-start(f32[2,384]{1,0:T(2,128)} %copy-done.37) | copy-start | bytes 9220
  581.0 97.5 %copy-start.36 = (f32[2,384]{1,0:T(2,128)S(1)}, f32[2,384]{1,0:T(2,128)}, u32[]{:S(2)}) copy-start(f32[2,384]{1,0:T(2,128)} %copy-done.35) | copy-start | bytes 9220
  581.0 97.5 %copy-start.40 = (f32[2,384]{1,0:T(2,128)S(1)}, f32[2,384]{1,0:T(2,128)}, u32[]{:S(2)}) copy-start(f32[2,384]{1,0:T(2,128)} %copy-done.39) | copy-start | bytes 9220
  (42 other events, 274.5 us)
Sparse Core Ops, SparseCore 0:
  14.7 40.1 all-gather.2
  125.8 47.8 reduce-scatter.2
  235.9 37.4 all-gather.4
  543.6 80.2 all-reduce.7
  626.3 47.1 reduce-scatter.4
  681.4 305.0 all-reduce.5
where the time goes:
time: 1010 us
  waiting for transfers between devices  454 us (45%)
  matrix products  354 us (35%)
  other arithmetic  76.2 us (8%)
  blocking collectives  64 us (6%)
  local copies, waits for them, and re-layouts  40.5 us (4%)
  between operations  14.8 us (1%)
    psum x1, waiting for transfers between devices, body(): lax.psum((grad_gain_one, grad_shift_one, grad_b_out, grad_gain_two, grad_...  262 us
    dot_general x6, matrix products, row_backward(): jnp.einsum('hqk,khe->qhe', score_grad, key_rows, preferred_element_type=j...  89.1 us
    dot_general x6, matrix products, row_backward(): jnp.einsum('hqk,qhe->khe', score_grad, query_block, preferred_element_typ...  87.3 us
    reduce_scatter x1, waiting for transfers between devices, body(): lax.psum_scatter(partial_out.astype(jnp.bfloat16), ('th', 'tw'), scatter_...  47.9 us
    reduce_scatter x1, waiting for transfers between devices, body(): lax.psum_scatter(grad_normed.astype(jnp.bfloat16), ('th', 'tw'), scatter_...  45.2 us
    psum x1, blocking collectives, body(): lax.psum((grad_gain_one, grad_shift_one, grad_b_out, grad_gain_two, grad_...  42.5 us
    all_gather x1, waiting for transfers between devices, body(): gathered = lax.all_gather(normed_low, ('th', 'tw'), axis=1, tiled=True)  40.1 us
    all_gather x1, waiting for transfers between devices, body(): grad_whole = lax.all_gather(grad_branch, ('th', 'tw'), axis=1, tiled=True)  37.6 us
  transfers between devices with their start and end apart: 6, of which 6 were waited for; matrix products, arithmetic and copies ran while one was open for 5% of the time, Pallas kernels for 0%

commit v1 on v0

v1 whole, which is shorter than its diff:
```python
import jax
import jax.numpy as jnp
from jax import lax
from jax.experimental import pallas as pl
from jax.experimental.pallas import tpu as pltpu
from jax.sharding import PartitionSpec as P

NT=(((1,),(1,)),((),())); NN=(((1,),(0,)),((),())); TN=(((0,),(0,)),((),()))
F32=jnp.float32; BF=jnp.bfloat16
BQ=256; BK=256; HD=64
def dot(a,b,d): return lax.dot_general(a,b,d,preferred_element_type=F32)

def fwd_kernel(lo_ref, hi_ref, q_ref, k_ref, v_ref, mq_ref, mk_ref, o_ref, lse_ref, m_ref, l_ref, acc_ref):
    i=pl.program_id(0)
    pairs=q_ref.shape[1]//128
    lane=lax.broadcasted_iota(jnp.int32,(1,128),1)
    halves=(lane<HD, lane>=HD)
    m_ref[...]=jnp.full(m_ref.shape,-1e30,F32)
    l_ref[...]=jnp.zeros_like(l_ref)
    acc_ref[...]=jnp.zeros_like(acc_ref)
    def body(j,_):
        ks=pl.ds(pl.multiple_of(j*BK,BK),BK)
        mk=mk_ref[ks,:]
        for p in range(pairs):
            cols=slice(p*128,(p+1)*128)
            qx=jnp.concatenate([q_ref[:,cols],mq_ref[...]],1)
            k2=k_ref[ks,cols]; v2=v_ref[ks,cols]
            ps=[]
            for e in range(2):
                h=2*p+e
                kx=jnp.concatenate([jnp.where(halves[e],k2,jnp.zeros_like(k2)),mk],1)
                s=dot(kx,qx,NT)
                m_old=m_ref[h:h+1,:]
                m_new=jnp.maximum(m_old,jnp.max(s,axis=0,keepdims=True))
                alpha=jnp.exp(m_old-m_new)
                pe=jnp.exp(s-m_new)
                l_ref[h:h+1,:]=l_ref[h:h+1,:]*alpha+jnp.sum(pe,axis=0,keepdims=True)
                m_ref[h:h+1,:]=m_new
                acc_ref[h*HD:(h+1)*HD,:]=acc_ref[h*HD:(h+1)*HD,:]*alpha
                ps.append(pe.astype(BF))
            vcat=jnp.concatenate([jnp.where(halves[0],v2,jnp.zeros_like(v2)),jnp.where(halves[1],v2,jnp.zeros_like(v2))],0)
            acc_ref[cols,:]+=dot(vcat,jnp.concatenate(ps,0),TN)
        return 0
    lax.fori_loop(lo_ref[i],hi_ref[i],body,0)
    for p in range(pairs):
        parts=[]
        for e in range(2):
            h=2*p+e
            parts.append(acc_ref[h*HD:(h+1)*HD,:]*(1.0/l_ref[h:h+1,:]))
        o_ref[:,p*128:(p+1)*128]=jnp.concatenate(parts,0).T.astype(BF)
    lse_ref[...]=m_ref[...]+jnp.log(jnp.maximum(l_ref[...],1e-37))

def attn_fwd(q,k,v,mq,mk,lo,hi):
    L,C=q.shape
    return pl.pallas_call(fwd_kernel,
        grid_spec=pltpu.PrefetchScalarGridSpec(num_scalar_prefetch=2,grid=(L//BQ,),
          in_specs=[pl.BlockSpec((BQ,C),lambda i,*_:(i,0)),pl.BlockSpec((L,C),lambda i,*_:(0,0)),pl.BlockSpec((L,C),lambda i,*_:(0,0)),
                    pl.BlockSpec((BQ,128),lambda i,*_:(i,0)),pl.BlockSpec((L,128),lambda i,*_:(0,0))],
          out_specs=[pl.BlockSpec((BQ,C),lambda i,*_:(i,0)),pl.BlockSpec((8,BQ),lambda i,*_:(0,i))],
          scratch_shapes=[pltpu.VMEM((8,BQ),F32),pltpu.VMEM((8,BQ),F32),pltpu.VMEM((C,BQ),F32)]),
        out_shape=[jax.ShapeDtypeStruct((L,C),BF),jax.ShapeDtypeStruct((8,L),F32)],
        name="attention_forward",
    )(lo,hi,q,k,v,mq,mk)

def bwd_kernel(lo_ref, hi_ref, q_ref, k_ref, v_ref, do_ref, o_ref, lse_ref, mq_ref, mk_ref, dq_ref, dk_ref, dv_ref, dk_acc, dv_acc, dq_acc, qcat, docat):
    i=pl.program_id(0); n=pl.num_programs(0)
    C=q_ref.shape[1]; pairs=C//128
    lane=lax.broadcasted_iota(jnp.int32,(1,128),1)
    halves=(lane<HD, lane>=HD)
    @pl.when(i==0)
    def _():
        dk_acc[...]=jnp.zeros_like(dk_acc); dv_acc[...]=jnp.zeros_like(dv_acc)
    dq_acc[...]=jnp.zeros_like(dq_acc)
    sel=(lax.broadcasted_iota(jnp.int32,(8,C),1)//HD==lax.broadcasted_iota(jnp.int32,(8,C),0)).astype(F32)
    delta=lax.dot_general(sel,do_ref[...].astype(F32)*o_ref[...].astype(F32),NT,precision=lax.Precision.HIGHEST,preferred_element_type=F32)
    for p in range(pairs):
        cols=slice(p*128,(p+1)*128)
        for e in range(2):
            q2=q_ref[:,cols]; d2=do_ref[:,cols]
            qcat[p,e*BQ:(e+1)*BQ,:]=jnp.where(halves[e],q2,jnp.zeros_like(q2))
            docat[p,e*BQ:(e+1)*BQ,:]=jnp.where(halves[e],d2,jnp.zeros_like(d2))
    lse=lse_ref[...]
    def body(j,_):
        ks=pl.ds(pl.multiple_of(j*BK,BK),BK)
        mk=mk_ref[ks,:]
        for p in range(pairs):
            cols=slice(p*128,(p+1)*128)
            qx=jnp.concatenate([q_ref[:,cols],mq_ref[...]],1)
            k2=k_ref[ks,cols]; v2=v_ref[ks,cols]; d2=do_ref[:,cols]
            ps=[]; dss=[]; kms=[]
            for e in range(2):
                h=2*p+e
                km=jnp.where(halves[e],k2,jnp.zeros_like(k2)); vm=jnp.where(halves[e],v2,jnp.zeros_like(v2))
                s=dot(jnp.concatenate([km,mk],1),qx,NT)
                pr=jnp.exp(s-lse[h:h+1,:])
                dp=dot(vm,d2,NT)
                ds=pr*(dp-delta[h:h+1,:])
                ps.append(pr.astype(BF)); dss.append(ds.astype(BF)); kms.append(km)
            dv_acc[ks,cols]+=dot(jnp.concatenate(ps,1),docat[p],NN)
            dk_acc[ks,cols]+=dot(jnp.concatenate(dss,1),qcat[p],NN)
            dq_acc[cols,:]+=dot(jnp.concatenate(kms,0),jnp.concatenate(dss,0),TN)
        return 0
    lax.fori_loop(lo_ref[i],hi_ref[i],body,0)
    dq_ref[...]=(dq_acc[...]*0.125).T.astype(BF)
    @pl.when(i==n-1)
    def _():
        dk_ref[...]=dk_acc[...].astype(BF); dv_ref[...]=dv_acc[...].astype(BF)

def attn_bwd(q,k,v,do,o,lse,mq,mk,lo,hi):
    L,C=q.shape
    blk=pl.BlockSpec((BQ,C),lambda i,*_:(i,0)); full=pl.BlockSpec((L,C),lambda i,*_:(0,0))
    return pl.pallas_call(bwd_kernel,
        grid_spec=pltpu.PrefetchScalarGridSpec(num_scalar_prefetch=2,grid=(L//BQ,),
          in_specs=[blk,full,full,blk,blk,pl.BlockSpec((8,BQ),lambda i,*_:(0,i)),pl.BlockSpec((BQ,128),lambda i,*_:(i,0)),pl.BlockSpec((L,128),lambda i,*_:(0,0))],
          out_specs=[blk,full,full],
          scratch_shapes=[pltpu.VMEM((L,C),F32),pltpu.VMEM((L,C),F32),pltpu.VMEM((C,BQ),F32),pltpu.VMEM((C//128,2*BQ,128),BF),pltpu.VMEM((C//128,2*BQ,128),BF)]),
        out_shape=[jax.ShapeDtypeStruct((L,C),BF)]*3,
        name="attention_backward",
    )(lo,hi,q,k,v,do,o,lse,mq,mk)

def seg_tables(seg):
    L=seg.shape[0]
    lane=jnp.arange(128,dtype=jnp.int32)[None,:]
    same=seg[:,None]==lane
    mk=same.astype(BF)
    mq=jnp.where(same|(lane>=8),0.0,-float(2**40)).astype(BF)
    first=seg[::BQ]; last=seg[BQ-1::BQ]
    lo=jnp.sum(seg[None,:]<first[:,None],axis=1,dtype=jnp.int32)//BK
    hi=(jnp.sum(seg[None,:]<=last[:,None],axis=1,dtype=jnp.int32)+BK-1)//BK
    return mq,mk,lo,hi

EPSILON = 1e-06


def layer_norm(field, norm_gain, norm_shift):
    average = jnp.mean(field, axis=-1, keepdims=True)
    centred = field - average
    spread = jnp.mean(centred * centred, axis=-1, keepdims=True)
    return centred * lax.rsqrt(spread + EPSILON) * norm_gain + norm_shift


def gelu_exact(field):
    return jax.nn.gelu(field, approximate=False)


SWAP = [(0, 1), (1, 0)]


def swap(value, axis):
    return lax.ppermute(value, axis, SWAP)


def in_order(mine, other, index, axis):
    return jnp.where(
        index == 0, jnp.concatenate([mine, other], axis), jnp.concatenate([other, mine], axis)
    )


def own_row(rows, tw):
    mine = lax.dynamic_index_in_dim(rows, tw, 0, keepdims=False)
    other = lax.dynamic_index_in_dim(rows, 1 - tw, 0, keepdims=False)
    return in_order(mine, swap(other, "tw"), tw, 0)


def back_rows(half, tw):
    quarter = half.shape[0] // 2
    mine = lax.dynamic_slice_in_dim(half, tw * quarter, quarter, 0)
    other = lax.dynamic_slice_in_dim(half, (1 - tw) * quarter, quarter, 0)
    got = swap(other, "tw")
    return jnp.where(tw == 0, jnp.stack([mine, got]), jnp.stack([got, mine]))


def whole_row(half, th):
    return in_order(half, swap(half, "th"), th, 0)


def sum_halves(partial, th):
    half = partial.shape[0] // 2
    mine = lax.dynamic_slice_in_dim(partial, th * half, half, 0)
    other = lax.dynamic_slice_in_dim(partial, (1 - th) * half, half, 0)
    return mine + swap(other.astype(BF), "th").astype(F32)


def mm(spec, a, b):
    return jnp.einsum(spec, a, b, preferred_element_type=F32)


def body(
    tokens,
    segment_ids,
    norm1_gain,
    norm1_shift,
    w_qkv,
    b_qv,
    w_out,
    b_out,
    norm2_gain,
    norm2_shift,
    w_up,
    b_up,
    w_down,
    b_down,
    cotangent,
):
    th, tw = lax.axis_index("th"), lax.axis_index("tw")
    d = tokens.shape[-1]
    mine = w_qkv.shape[2]
    inputs = own_row(tokens, tw).astype(F32)
    w_qkv_other = swap(w_qkv, "tw")
    w_heads = jnp.concatenate([w_qkv, w_qkv_other], 2)
    b_heads = jnp.concatenate([b_qv, swap(b_qv, "tw")], 1)
    w_out_heads = jnp.concatenate([w_out, swap(w_out, "tw")], 0)
    cot = own_row(cotangent, tw)
    seg = lax.dynamic_index_in_dim(segment_ids, tw, 0, keepdims=False)
    tables = seg_tables(seg)

    normed_one, norm_one_back = jax.vjp(layer_norm, inputs, norm1_gain, norm1_shift)
    normed_row = whole_row(normed_one.astype(BF), th)
    query = (mm("ld,de->le", normed_row, w_heads[0]) + b_heads[0]).astype(BF) * BF(0.125)
    key = mm("ld,de->le", normed_row, w_heads[1]).astype(BF)
    value = (mm("ld,de->le", normed_row, w_heads[2]) + b_heads[1]).astype(BF)
    attended, totals = attn_fwd(query, key, value, *tables)
    middle = inputs + sum_halves(mm("le,ed->ld", attended, w_out_heads), th) + b_out
    normed_two, norm_two_back = jax.vjp(layer_norm, middle, norm2_gain, norm2_shift)
    second_low = normed_two.astype(BF)
    hidden_pre = mm("ld,df->lf", second_low, w_up) + b_up
    activated, gelu_back = jax.vjp(gelu_exact, hidden_pre)
    active_low = activated.astype(BF)
    grad_w_down = mm("lf,ld->fd", active_low, cot)
    grad_active = mm("ld,fd->lf", cot, w_down)
    grad_hidden = gelu_back(grad_active)[0].astype(BF)
    grad_w_up = mm("ld,lf->df", second_low, grad_hidden)
    big = lax.psum((grad_w_up.astype(BF), grad_w_down.astype(BF)), ("dp", "th", "tw"))
    block_out = middle + (mm("lf,fd->ld", active_low, w_down) + b_down)
    block_out = back_rows(block_out.astype(BF), tw)
    upstream = cot.astype(F32)
    grad_b_down = jnp.sum(upstream, axis=0)
    grad_b_up = jnp.sum(grad_hidden.astype(F32), axis=0)
    grad_normed_two = mm("lf,df->ld", grad_hidden, w_up)
    grad_mid_norm, grad_gain_two, grad_shift_two = norm_two_back(grad_normed_two)
    grad_middle = upstream + grad_mid_norm
    grad_branch = grad_middle.astype(BF)
    grad_b_out = jnp.sum(grad_branch.astype(F32), axis=0)
    grad_whole = whole_row(grad_branch, th)
    grad_heads = mm("ld,ed->le", grad_whole, w_out_heads).astype(BF)
    grad_w_out = mm("le,ld->ed", attended, grad_whole)
    dq, dk, dv = attn_bwd(query, key, value, grad_heads, attended, totals, *tables)
    grad_w_qkv = jnp.stack([mm("ld,le->de", normed_row, g) for g in (dq, dk, dv)])
    grad_normed = (
        mm("le,de->ld", dq, w_heads[0]) + mm("le,de->ld", dk, w_heads[1]) + mm("le,de->ld", dv, w_heads[2])
    )
    grad_tile = sum_halves(grad_normed, th)
    grad_inputs, grad_gain_one, grad_shift_one = norm_one_back(grad_tile)
    grad_tokens = back_rows((grad_middle + grad_inputs).astype(BF), tw)

    def reduce_heads(grad, axis):
        own = lax.slice_in_dim(grad, 0, mine, axis=axis)
        other = lax.slice_in_dim(grad, mine, 2 * mine, axis=axis)
        return (own + swap(other.astype(BF), "tw").astype(F32)).astype(BF)

    heads = lax.psum((reduce_heads(grad_w_qkv, 2), reduce_heads(grad_w_out, 0)), "dp")
    grad_b = jnp.stack([jnp.sum(dq.astype(F32), 0), jnp.sum(dv.astype(F32), 0)])
    place = jnp.zeros((2, d), F32)
    place = lax.dynamic_update_slice(place, grad_b[:, :mine], (0, (2 * th + tw) * mine))
    place = lax.dynamic_update_slice(place, grad_b[:, mine:], (0, (2 * th + 1 - tw) * mine))
    vectors = (grad_gain_one, grad_shift_one, grad_b_out, grad_gain_two, grad_shift_two, grad_b_down, grad_b_up, place.reshape(-1))
    small = lax.psum(jnp.concatenate(vectors), ("dp", "th", "tw"))
    small_b_qv = lax.dynamic_slice_in_dim(small[-2 * d :].reshape(2, d), (2 * th + tw) * mine, mine, 1)
    return (
        block_out,
        grad_tokens,
        small[:d],
        small[d : 2 * d],
        heads[0].astype(F32),
        small_b_qv,
        heads[1].astype(F32),
        small[2 * d : 3 * d],
        small[3 * d : 4 * d],
        small[4 * d : 5 * d],
        big[0].astype(F32),
        small[6 * d : -2 * d],
        big[1].astype(F32),
        small[5 * d : 6 * d],
    )


def solution(mesh):
    return jax.shard_map(
        body,
        mesh=mesh,
        in_specs=(
            P("dp", ("th", "tw"), None),
            P("dp", None),
            P(),
            P(),
            P(None, None, ("th", "tw")),
            P(None, ("th", "tw")),
            P(("th", "tw"), None),
            P(),
            P(),
            P(),
            P(),
            P(),
            P(),
            P(),
            P("dp", ("th", "tw"), None),
        ),
        out_specs=(
            P("dp", ("th", "tw"), None),
            P("dp", ("th", "tw"), None),
            P(),
            P(),
            P(None, None, ("th", "tw")),
            P(None, ("th", "tw")),
            P(("th", "tw"), None),
            P(),
            P(),
            P(),
            P(),
            P(),
            P(),
            P(),
        ),
        check_vma=False,
    )
```

time: 1010 us -> 553 us (0.55)
  matrix products: 354 us -> 112 us
  waiting for transfers between devices: 454 us -> 226 us
  Pallas kernels: 0 us -> 62.9 us
  other arithmetic: 76.2 us -> 49.6 us
  local copies, waits for them, and re-layouts: 40.5 us -> 20.8 us
  blocking collectives: 64 us -> 48.9 us
  starting transfers between devices: 0.25 us -> 11.5 us
    dot_general x54 -> x18, matrix products: 354 us -> 112 us  [mm(): return jnp.einsum(spec, a, b, preferred_element_type=F32)]
    psum x2, waiting for transfers between devices: 283 us -> 188 us  [the longest x1 188 us: body(): lax.psum((grad_w_up.astype(BF), grad_w_down.astype(BF)), ('dp', 'th', 'tw'))]
    reduce_scatter x2 -> x0, waiting for transfers between devices: 93.1 us -> none  [the longest x1 47.9 us: body(): lax.psum_scatter(partial_out.astype(jnp.bfloat16), ('th', 'tw'), scatter_...]
    all_gather x2 -> x0, waiting for transfers between devices: 77.7 us -> none  [the longest x1 40.1 us: body(): gathered = lax.all_gather(normed_low, ('th', 'tw'), axis=1, tiled=True)]
    pallas_call x0 -> x2, Pallas kernels: none -> 62.9 us  [the longest x1 35.2 us: attn_bwd(): pl.pallas_call(bwd_kernel, grid_spec=pltpu.PrefetchScalarGridSpec(num_sca...]
    ppermute x0 -> x13, waiting for transfers between devices: none -> 37.7 us  [swap(): return lax.ppermute(value, axis, SWAP)]
    psum x2 -> x1, blocking collectives: 64 us -> 48.9 us  [body(): small = lax.psum(jnp.concatenate(vectors), ('dp', 'th', 'tw'))]
    while x28 -> x0, local copies, waits for them, and re-layouts: 13.9 us -> none
  transfers between devices with their start and end apart: 6 -> 15, of which waited for: 6 -> 4; matrix products, arithmetic and copies ran while one was open for 5% -> 21% of each run, Pallas kernels for 0% -> 6%
where the time goes in v1:
time: 553 us; the launch traced here: 547 us
  waiting for transfers between devices  226 us (41%)
  matrix products  112 us (20%)
  Pallas kernels  62.9 us (11%)
  other arithmetic  49.6 us (9%)
  blocking collectives  48.9 us (9%)
  local copies, waits for them, and re-layouts  20.8 us (4%)
  between operations  15.4 us (3%)
  starting transfers between devices  11.5 us (2%)
    psum x1, waiting for transfers between devices, body(): lax.psum((grad_w_up.astype(BF), grad_w_down.astype(BF)), ('dp', 'th', 'tw'))  188 us
    dot_general x18, matrix products, mm(): return jnp.einsum(spec, a, b, preferred_element_type=F32)  112 us
    psum x1, blocking collectives, body(): small = lax.psum(jnp.concatenate(vectors), ('dp', 'th', 'tw'))  48.9 us
    ppermute x13, waiting for transfers between devices, swap(): return lax.ppermute(value, axis, SWAP)  37.7 us
    pallas_call x1, Pallas kernels, attn_bwd(): pl.pallas_call(bwd_kernel, grid_spec=pltpu.PrefetchScalarGridSpec(num_sca...  35.2 us
    pallas_call x1, Pallas kernels, attn_fwd(): pl.pallas_call(fwd_kernel, grid_spec=pltpu.PrefetchScalarGridSpec(num_sca...  27.7 us
    ppermute x13, starting transfers between devices, swap(): return lax.ppermute(value, axis, SWAP)  11.1 us
  transfers between devices with their start and end apart: 15, of which 4 were waited for; matrix products, arithmetic and copies ran while one was open for 21% of the time, Pallas kernels for 6%

profile of v1, /device:TPU:0, one launch (start us, length us, event | category | flops | bytes accessed | tf_op | source)
XLA Modules:
  0.0 547.2 jit_solution(5924702265510454714)
XLA Ops:
  14.8 11.0 %collective-permute-done = bf16[384,768]{1,0:T(8,128)(2,1)S(1)} collective-permute-done((bf16[384,768]{1,0:T(8,128)(2,1)S(1)}, bf16[384,768]{1,0:T(8,128)(2,1)S(1)}, u32[]{:S(2)}, u32[]{:S(2)}) %collective-permute-start) | collective-permute-done | bytes 589856 | tf_op jit(solution)/shard_map/ppermute | solution.py:150
  34.6 15.9 %collective-permute-done.2 = bf16[3,768,192]{1,2,0:T(8,128)(2,1)} collective-permute-done((bf16[3,768,192]{1,2,0:T(8,128)(2,1)}, bf16[3,768,192]{1,2,0:T(8,128)(2,1)}, u32[]{:S(2)}, u32[]{:S(2)}) %collective-permute-start.2) | collective-permute-done | bytes 884768 | tf_op jit(solution)/shard_map/ppermute | solution.py:150
  51.7 5.4 convolution_convert_fusion.3.k_ref
  57.1 4.9 fusion.11.v_ref
  62.0 4.8 fusion.14.q_ref
  66.9 27.7 %attention_forward.1 = (bf16[1536,384]{1,0:T(8,128)(2,1)}, f32[8,1536]{1,0:T(8,128)}) custom-call(s32[6]{0:T(128)} %get-tuple-element.71.lo_ref, s32[6]{0:T(128)} %get-tuple-element.70.hi_ref, bf16[1536,384]{1,0:T(8,128)(2,1)} %fusion.14.q_ref, bf16[1536,384]{1,0:T(8,128)(2,1)} %convolution_convert_fusion.3.k_ref, bf16[1536,384]{1,0:T(8,128)(2,1)} %fusion.11.v_ref, ...), custom_call_target="tpu_custom_call" | custom-call | tf_op jit(solution)/shard_map/attention_forward/pallas_call | solution.py:55
  106.0 28.0 %multiply_convert_fusion = (bf16[768,3072]{1,0:T(8,128)(2,1)}, f32[768,3072]{1,0:T(8,128)}, f32[768,3072]{1,0:T(8,128)}) fusion(f32[3072]{0:T(1024)S(1)} %copy-done.48, bf16[768,3072]{1,0:T(8,128)(2,1)} %param.25, f32[768,768]{1,0:T(8,128)S(1)} %get-tuple-element.47, f32[768]{0:T(1024)S(1)} %copy-done.50, f32[768]{0:T(1024)S(1)} %copy-done.43, ...), kind=kOutput, calls=%fused_computation.4 | convolution fusion | flops 3782541312 | bytes 30695424 | tf_op jit(solution)/shard_map/ld,df->lf/dot_general | solution.py:185
  134.0 13.7 %convert_reduce_fusion = (f32[3072]{0:T(1024)}, bf16[768,3072]{1,0:T(8,128)(2,1)S(1)}) fusion(f32[768,3072]{1,0:T(8,128)} %get-tuple-element.45, bf16[3072,768]{1,0:T(8,128)(2,1)} %param.27, bf16[384,768]{1,0:T(8,128)(2,1)} %collective-permute-done.7, bf16[384,768]{1,0:T(8,128)(2,1)S(1)} %copy-done.14, pred[]{:T(512)S(6)} %eq.10, ...), kind=kOutput, calls=%fused_computation.2 | convolution fusion | flops 3669292032 | bytes 29515776 | tf_op jit(solution)/shard_map/ld,fd->lf/dot_general | solution.py:185
  147.7 4.8 multiply_reduce_fusion
  153.5 4.3 convert_reduce_fusion.5
  157.8 8.7 %add_convert_fusion.2 = bf16[768,768]{1,0:T(8,128)(2,1)} fusion(f32[768,768]{1,0:T(8,128)S(1)} %get-tuple-element.47, bf16[768,3072]{1,0:T(8,128)(2,1)} %get-tuple-element.44, bf16[3072,768]{1,0:T(8,128)(2,1)} %param.27, f32[768]{0:T(1024)S(1)} %copy-done.49), kind=kOutput, calls=%fused_computation.58 | convolution fusion | flops 3625648128 | bytes 12979200 | tf_op jit(solution)/shard_map/lf,fd->ld/dot_general | solution.py:185
  172.2 4.9 convolution_convert_fusion.2.do_ref
  177.1 35.2 %attention_backward.1 = (bf16[1536,384]{1,0:T(8,128)(2,1)}, bf16[1536,384]{1,0:T(8,128)(2,1)}, bf16[1536,384]{1,0:T(8,128)(2,1)}) custom-call(s32[6]{0:T(128)} %get-tuple-element.71.lo_ref, s32[6]{0:T(128)} %get-tuple-element.70.hi_ref, bf16[1536,384]{1,0:T(8,128)(2,1)} %fusion.14.q_ref, bf16[1536,384]{1,0:T(8,128)(2,1)} %convolution_convert_fusion.3.k_ref, ...), custom_call_target="tpu_custom_call" | custom-call | tf_op jit(solution)/shard_map/attention_backward/pallas_call | solution.py:112
  212.3 3.9 convolution_bitcast_fusion.1
  216.3 3.6 convolution_bitcast_fusion.2
  225.8 6.4 %convolution_convert_fusion.1 = bf16[768,3072]{1,0:T(8,128)(2,1)} fusion(bf16[768,3072]{1,0:T(8,128)(2,1)S(1)} %bitcast.56, f32[768,768]{1,0:T(8,128)S(1)} %get-tuple-element.47, f32[768]{0:T(1024)S(1)} %copy-done.51, f32[768]{0:T(1024)S(1)} %copy-done.44, f32[768]{0:T(1024)S(1)} %copy-done.39, f32[768]{0:T(1024)S(1)} %broadcast_multiply_fusion), kind=kOutput, calls=%fused_computation.19 | convolution fusion | flops 3629187072 | bytes 11808768 | tf_op jit(solution)/shard_map/ld,lf->df/dot_general | solution.py:185
  235.7 10.8 %collective-permute-done.11 = bf16[3,768,192]{1,2,0:T(8,128)(2,1)S(1)} collective-permute-done((bf16[3,768,192]{1,2,0:T(8,128)(2,1)S(1)}, bf16[3,768,192]{1,2,0:T(8,128)(2,1)S(1)}, u32[]{:S(2)}, u32[]{:S(2)}) %collective-permute-start.11) | collective-permute-done | bytes 884768 | tf_op jit(solution)/shard_map/ppermute | solution.py:150
  248.0 8.8 %convolution_convert_fusion = bf16[3072,768]{1,0:T(8,128)(2,1)} fusion(bf16[768,3072]{1,0:T(8,128)(2,1)} %get-tuple-element.44, bf16[384,768]{1,0:T(8,128)(2,1)} %collective-permute-done.7, bf16[384,768]{1,0:T(8,128)(2,1)S(1)} %copy-done.14, pred[]{:T(512)S(6)} %eq.10), kind=kOutput, calls=%fused_computation.18 | convolution fusion | flops 3631546368 | bytes 10616833 | tf_op jit(solution)/shard_map/lf,ld->fd/dot_general | solution.py:185
  271.5 4.1 fusion.17
  275.6 3.6 fusion.42
  283.4 48.9 %psum.35 = f32[9216]{0:T(1024)S(1)} all-reduce(f32[9216]{0:T(1024)S(1)} %constant_dynamic-update-slice_fusion.5), channel_id=1, replica_groups=mesh['dp'=8,'th'=2,'tw'=2] {'dp','th','tw'}, use_global_device_ids=true, to_apply=%region_19.20 | all-reduce | flops 9216 | bytes 73728 | tf_op jit(solution)/shard_map/psum | solution.py:267
  339.7 188.1 %all-reduce.5.cloned.1.call-done = (bf16[768,3072]{1,0:T(8,128)(2,1)}, bf16[3072,768]{1,0:T(8,128)(2,1)}) async-done(((bf16[768,3072]{1,0:T(8,128)(2,1)}, bf16[3072,768]{1,0:T(8,128)(2,1)}), (bf16[768,3072]{1,0:T(8,128)(2,1)}, bf16[3072,768]{1,0:T(8,128)(2,1)})) %all-reduce.5.cloned.1.call-update) | async-done | bytes 9437200 | tf_op jit(solution)/shard_map/psum | solution.py:233
  527.8 7.5 %convert_element_type.139 = f32[768,3072]{1,0:T(8,128)} convert(bf16[768,3072]{1,0:T(8,128)(2,1)} %get-tuple-element.34) | non-fusion elementwise | flops 2359296 | bytes 14155776 | tf_op jit(solution)/shard_map/convert_element_type | solution.py:280
  535.3 4.5 convert_element_type.141
  (216 shorter events, 72.0 us)
Async XLA Ops:
  7.2 328.2 %all-reduce.7.cloned.1.call-start = ((), (), s32[]{:S(2)}) async-start(), calls=%async_computation.1 | async-start | bytes 2359296 | tf_op jit(solution)/shard_map/psum | solution.py:261
  7.3 19.6 %copy-start.32 = (f32[768]{0:T(1024)S(1)}, f32[768]{0:T(1024)}, u32[]{:S(2)}) copy-start(f32[768]{0:T(1024)} %param.17) | copy-start | bytes 9220
  7.3 19.6 %copy-start.41 = (f32[768]{0:T(1024)S(1)}, f32[768]{0:T(1024)}, u32[]{:S(2)}) copy-start(f32[768]{0:T(1024)} %param.18) | copy-start | bytes 9220
  8.6 93.7 %copy-start.2 = (bf16[384,768]{1,0:T(8,128)(2,1)}, bf16[384,768]{1,0:T(8,128)(2,1)S(1)}, u32[]{:S(2)}) copy-start(bf16[384,768]{1,0:T(8,128)(2,1)S(1)} %get-tuple-element.57) | copy-start | bytes 1769476
  8.6 17.2 %collective-permute-start = (bf16[384,768]{1,0:T(8,128)(2,1)S(1)}, bf16[384,768]{1,0:T(8,128)(2,1)S(1)}, u32[]{:S(2)}, u32[]{:S(2)}) collective-permute-start(bf16[384,768]{1,0:T(8,128)(2,1)S(1)} %get-tuple-element.56), channel_id=1, source_target_pairs={{0,1},{1,0},{2,3},{3,2},{4,5},{5,4},{6,7},{7,6},{8,9},{9,8},{10,11... | collective-permute-start | bytes 1769480 | tf_op jit(solution)/shard_map/ppermute | solution.py:150
  11.7 21.0 %collective-permute-start.3 = (f32[2,192]{1,0:T(2,128)S(1)}, f32[2,192]{1,0:T(2,128)}, u32[]{:S(2)}, u32[]{:S(2)}) collective-permute-start(f32[2,192]{1,0:T(2,128)S(1)} %copy-done.47), channel_id=1, source_target_pairs={{0,1},{1,0},{2,3},{3,2},{4,5},{5,4},{6,7},{7,6},{8,9},{9,8},{10,11... | collective-permute-start | bytes 4616 | tf_op jit(solution)/shard_map/ppermute | solution.py:150
  11.7 21.8 %collective-permute-start.4 = (bf16[192,768]{1,0:T(8,128)(2,1)}, bf16[192,768]{1,0:T(8,128)(2,1)}, u32[]{:S(2)}, u32[]{:S(2)}) collective-permute-start(bf16[192,768]{1,0:T(8,128)(2,1)} %param.21), channel_id=1, source_target_pairs={{0,1},{1,0},{2,3},{3,2},{4,5},{5,4},{6,7},{7,6},{8,9},{9,8},{10,11... | collective-permute-start | bytes 884744 | tf_op jit(solution)/shard_map/ppermute | solution.py:150
  13.7 36.7 %collective-permute-start.2 = (bf16[3,768,192]{1,2,0:T(8,128)(2,1)}, bf16[3,768,192]{1,2,0:T(8,128)(2,1)}, u32[]{:S(2)}, u32[]{:S(2)}) collective-permute-start(bf16[3,768,192]{1,2,0:T(8,128)(2,1)} %param.19), channel_id=1, source_target_pairs={{0,1},{1,0},{2,3},{3,2},{4,5},{5,4},{6,7},{7,6},{8,9},{9,8},{10,11... | collective-permute-start | bytes 2654216 | tf_op jit(solution)/shard_map/ppermute | solution.py:150
  25.8 76.5 %copy-start.9 = (bf16[384,768]{1,0:T(8,128)(2,1)}, bf16[384,768]{1,0:T(8,128)(2,1)S(1)}, u32[]{:S(2)}) copy-start(bf16[384,768]{1,0:T(8,128)(2,1)S(1)} %collective-permute-done) | copy-start | bytes 1769476
  28.5 23.2 %collective-permute-start.1 = (bf16[768,768]{1,0:T(8,128)(2,1)}, bf16[768,768]{1,0:T(8,128)(2,1)}, u32[]{:S(2)}, u32[]{:S(2)}) collective-permute-start(bf16[768,768]{1,0:T(8,128)(2,1)} %fusion.16), channel_id=1, source_target_pairs={{0,2},{2,0},{1,3},{3,1},{4,6},{6,4},{5,7},{7,5},{8,10},{10,8},{9,1... | collective-permute-start | bytes 3538952 | tf_op jit(solution)/shard_map/ppermute | solution.py:150
  34.5 60.1 %copy-start.22 = (bf16[384,768]{1,0:T(8,128)(2,1)}, bf16[384,768]{1,0:T(8,128)(2,1)S(1)}, u32[]{:S(2)}) copy-start(bf16[384,768]{1,0:T(8,128)(2,1)S(1)} %constant_dynamic-update-slice_fusion.2) | copy-start | bytes 1769476
  97.4 4.8 collective-permute-start.5
  100.5 33.4 %collective-permute-start.7 = (bf16[384,768]{1,0:T(8,128)(2,1)}, bf16[384,768]{1,0:T(8,128)(2,1)}, u32[]{:S(2)}, u32[]{:S(2)}) collective-permute-start(bf16[384,768]{1,0:T(8,128)(2,1)} %get-tuple-element.53), channel_id=1, source_target_pairs={{0,1},{1,0},{2,3},{3,2},{4,5},{5,4},{6,7},{7,6},{8,9},{9,8},{10,11... | collective-permute-start | bytes 1769480 | tf_op jit(solution)/shard_map/ppermute | solution.py:150
  102.3 45.4 %slice-start = ((s8[4718592]{0:T(1024)(128)(4,1)}), s8[4194304]{0:T(1024)(128)(4,1)S(1)}, s32[]{:S(2)}) async-start(s8[4718592]{0:T(1024)(128)(4,1)} %bitcast.53), calls=%async_computation.2 | async-start | bytes 8388608
  106.0 46.6 %copy-start.38 = (f32[768]{0:T(1024)}, f32[768]{0:T(1024)S(1)}, u32[]{:S(2)}) copy-start(f32[768]{0:T(1024)S(1)} %fusion.31) | copy-start | bytes 9220
  106.0 28.0 %copy-start.14 = (bf16[384,768]{1,0:T(8,128)(2,1)S(1)}, bf16[384,768]{1,0:T(8,128)(2,1)}, u32[]{:S(2)}) copy-start(bf16[384,768]{1,0:T(8,128)(2,1)} %get-tuple-element.52) | copy-start | bytes 1769476
  106.0 41.7 %slice-start.1 = ((s8[4718592]{0:T(1024)(128)(4,1)}), s8[524288]{0:T(1024)(128)(4,1)S(1)}, s32[]{:S(2)}) async-start(s8[4718592]{0:T(1024)(128)(4,1)} %bitcast.53), calls=%async_computation.3 | async-start | bytes 1048576
  157.8 8.7 %collective-permute-start.8 = (bf16[768,768]{1,0:T(8,128)(2,1)}, bf16[768,768]{1,0:T(8,128)(2,1)}, u32[]{:S(2)}, u32[]{:S(2)}) collective-permute-start(bf16[768,768]{1,0:T(8,128)(2,1)} %get-tuple-element.39), channel_id=1, source_target_pairs={{0,2},{2,0},{1,3},{3,1},{4,6},{6,4},{5,7},{7,5},{8,10},{10,8},{9,1... | collective-permute-start | bytes 3538952 | tf_op jit(solution)/shard_map/ppermute | solution.py:150
  171.9 61.7 %collective-permute-start.12 = (bf16[192,768]{1,0:T(8,128)(2,1)}, bf16[192,768]{1,0:T(8,128)(2,1)}, u32[]{:S(2)}, u32[]{:S(2)}) collective-permute-start(bf16[192,768]{1,0:T(8,128)(2,1)} %slice.155), channel_id=1, source_target_pairs={{0,1},{1,0},{2,3},{3,2},{4,5},{5,4},{6,7},{7,6},{8,9},{9,8},{10,11... | collective-permute-start | bytes 884744 | tf_op jit(solution)/shard_map/ppermute | solution.py:150
  224.0 22.5 %collective-permute-start.11 = (bf16[3,768,192]{1,2,0:T(8,128)(2,1)S(1)}, bf16[3,768,192]{1,2,0:T(8,128)(2,1)S(1)}, u32[]{:S(2)}, u32[]{:S(2)}) collective-permute-start(bf16[3,768,192]{1,2,0:T(8,128)(2,1)S(1)} %slice.154), channel_id=1, source_target_pairs={{0,1},{1,0},{2,3},{3,2},{4,5},{5,4},{6,7},{7,6},{8,9},{9,8},{10,11... | collective-permute-start | bytes 2654216 | tf_op jit(solution)/shard_map/ppermute | solution.py:150
  233.3 32.8 %collective-permute-start.6 = (bf16[384,768]{1,0:T(8,128)(2,1)}, bf16[384,768]{1,0:T(8,128)(2,1)}, u32[]{:S(2)}, u32[]{:S(2)}) collective-permute-start(bf16[384,768]{1,0:T(8,128)(2,1)} %get-tuple-element.55), channel_id=1, source_target_pairs={{0,1},{1,0},{2,3},{3,2},{4,5},{5,4},{6,7},{7,6},{8,9},{9,8},{10,11... | collective-permute-start | bytes 1769480 | tf_op jit(solution)/shard_map/ppermute | solution.py:150
  247.7 280.2 %all-reduce.5.cloned.1.call-start = ((), (), s32[]{:S(2)}) async-start(), calls=%async_computation | async-start | bytes 18874368 | tf_op jit(solution)/shard_map/psum | solution.py:233
  266.1 5.3 collective-permute-start.9
  281.5 52.7 %collective-permute-start.10 = (bf16[384,768]{1,0:T(8,128)(2,1)S(1)}, bf16[384,768]{1,0:T(8,128)(2,1)S(1)}, u32[]{:S(2)}, u32[]{:S(2)}) collective-permute-start(bf16[384,768]{1,0:T(8,128)(2,1)S(1)} %get-tuple-element.51), channel_id=1, source_target_pairs={{0,1},{1,0},{2,3},{3,2},{4,5},{5,4},{6,7},{7,6},{8,9},{9,8},{10,11... | collective-permute-start | bytes 1769480 | tf_op jit(solution)/shard_map/ppermute | solution.py:150
  (48 other events, 188.7 us)
Sparse Core Ops, SparseCore 0:
  247.8 82.0 all-reduce.6
  337.4 190.4 all-reduce.4

commit v2 on v1

--- a/solution.py
+++ b/solution.py
@@ -1,3 +1,5 @@
+import functools
+
 import jax
 import jax.numpy as jnp
 from jax import lax
@@ -129,6 +131,276 @@
     hi=(jnp.sum(seg[None,:]<=last[:,None],axis=1,dtype=jnp.int32)+BK-1)//BK
     return mq,mk,lo,hi
 
+
+TT=256; FC=512
+LAG=2; GLAG=2; HLAG=2; HC=3; HSP=2
+
+def bits_of(dp): return dp.bit_length()-1
+
+def big_plan(dp,rows):
+    n=bits_of(dp)
+    orders=(["tw"]+list(range(n)),[0,"tw"]+list(range(1,n)),[1,2,0,"tw"]+list(range(3,n)))
+    unit=16<<(n+1)
+    units=rows//unit
+    third=max(1,units//4)
+    shares=[units-units//3-third,units//3,third]
+    return streams(orders,shares,unit)
+
+def head_plan(dp,rows):
+    n=bits_of(dp)
+    orders=(["tw"]+list(range(n)),[1,2,0,"tw"]+list(range(3,n)))
+    unit=16<<n
+    units=rows//unit
+    low=max(1,units//6)
+    return streams(orders,[units-low,low],unit)
+
+def streams(orders,shares,unit):
+    out=[]; start=0
+    for order,share in zip(orders,shares):
+        out.append((order,start,share*unit)); start+=share*unit
+    return out
+
+class Peers:
+    def __init__(self):
+        self.dp=lax.axis_index("dp"); self.th=lax.axis_index("th"); self.tw=lax.axis_index("tw")
+    def bit(self,axis):
+        return self.tw if axis=="tw" else (self.dp//(1<<axis))%2
+    def peer(self,axis):
+        if axis=="tw": return {"tw":1-self.tw}
+        if axis=="th": return {"th":1-self.th}
+        return {"dp":self.dp+(1-2*self.bit(axis))*(1<<axis)}
+
+def send(src,dst,ssem,rsem,peer):
+    return pltpu.make_async_remote_copy(src,dst,ssem,rsem,device_id=peer,device_id_type=pl.DeviceIdType.MESH)
+
+def barrier(p,axes):
+    sem=pltpu.get_barrier_semaphore()
+    for a in axes:
+        pl.semaphore_signal(sem,inc=1,device_id=p.peer(a),device_id_type=pl.DeviceIdType.MESH)
+    pl.semaphore_wait(sem,len(axes))
+
+def halves(p,order,row,rows,keep_tw=False):
+    out=[]
+    for axis in order:
+        if keep_tw and axis=="tw": out.append((row,row,rows)); continue
+        rows//=2; bit=p.bit(axis)
+        out.append((row+(1-bit)*rows,row+bit*rows,rows)); row=row+bit*rows
+    return out
+def al(x): return x if isinstance(x,int) else pl.multiple_of(x,16)
+def rows_at(row,n): return pl.ds(al(row),n)
+
+def ffn_kernel(dp,n2,n2T,cot,cotT,wu,wd,bu,bo,gn,gb,red,act,gh,dw,chip_recv,*rest):
+    CH=dw.shape[0]; D=n2.shape[1]; T=n2.shape[0]
+    plan=big_plan(dp,dw.shape[2]); n=len(plan[0][0]); K=len(plan)
+    recv=[rest[k*n:(k+1)*n] for k in range(K)]
+    send_sem,recv_sem,chip_send,chip_got=rest[K*n:]
+    p=Peers(); g=pl.program_id(0)
+    regs=[halves(p,*s) for s in plan]
+    def copy(k,s,c):
+        out,_,nr=regs[k][s]
+        return send(dw.at[c,p.th,rows_at(out,nr),:],recv[k][s].at[c],send_sem.at[k,s,c],recv_sem.at[k,s,c],p.peer(plan[k][0][s]))
+    def chip_copy(c):
+        return send(dw.at[c,1-p.th],chip_recv.at[c],chip_send.at[c],chip_got.at[c],p.peer("th"))
+    @pl.when(g==0)
+    def _():
+        barrier(p,["th"]+plan[0][0])
+        bo[...]=jnp.zeros_like(bo); gn[...]=jnp.zeros_like(gn)
+    for s in reversed(range(n)):
+        c=g-1-LAG*(s+1)
+        @pl.when((c>=0)&(c<CH))
+        def _():
+            out=0
+            for k in range(K):
+                copy(k,s,c).wait_recv()
+                _,kr,nr=regs[k][s]
+                at=(c,p.th,rows_at(kr,nr),slice(None))
+                new=dw[at].astype(F32)+recv[k][s][c].astype(F32)
+                if s<n-1: dw[at]=new.astype(BF)
+                else:
+                    red[c,out:out+nr,:]=new.astype(BF); out+=nr
+    for s in reversed(range(n)):
+        c=g-1-LAG*s
+        @pl.when((c>=0)&(c<CH))
+        def _():
+            for k in range(K): copy(k,s,c).start()
+    @pl.when(g<CH)
+    def _():
+        gsum=jnp.zeros((1,FC),F32)
+        for t in range(T//TT):
+            r=slice(t*TT,(t+1)*TT)
+            h=dot(n2[r,:],wu[...],NN)+bu[...]
+            ga=dot(cot[r,:],wd[...],NT)
+            cdf=0.5*(1.0+lax.erf(h*(0.5**0.5)))
+            a=(h*cdf).astype(BF)
+            gr=(ga*(cdf+h*(jnp.exp(h*h*-0.5)*0.3989422804014327))).astype(BF)
+            act[r,:]=a; gh[r,:]=gr
+            gsum+=jnp.sum(gr.astype(F32),0,keepdims=True)
+        gb[...]=gsum
+        for t in range(D//TT):
+            r=slice(t*TT,(t+1)*TT)
+            for m,(lhs,rhs) in enumerate(((n2T,gh),(cotT,act))):
+                x=dot(lhs[r,:],rhs[...],NN).astype(BF)
+                for q in range(FC//128): dw[g,m,q*D+t*TT:q*D+(t+1)*TT,:]=x[:,q*128:(q+1)*128]
+        chip_copy(g).start()
+        for t in range(T//TT):
+            r=slice(t*TT,(t+1)*TT)
+            bo[r,:]+=dot(act[r,:],wd[...],NN)
+            gn[r,:]+=dot(gh[r,:],wu[...],NT)
+        chip_copy(g).wait_recv()
+        def add(q,_):
+            r=rows_at(q*TT,TT)
+            dw[g,p.th,r,:]=(dw[g,p.th,r,:].astype(F32)+chip_recv[g,r,:].astype(F32)).astype(BF)
+            return 0
+        lax.fori_loop(0,dw.shape[2]//TT,add,0)
+    @pl.when(g==CH+LAG*n)
+    def _():
+        def drain(c,_):
+            chip_copy(c).wait_send()
+            for k in range(K):
+                for s in range(n): copy(k,s,c).wait_send()
+            return 0
+        lax.fori_loop(0,CH,drain,0)
+
+def ffn(dp,n2,n2T,cot,cotT,wu,wd,bu):
+    T,D=n2.shape; FF=wu.shape[1]; CH=FF//FC; R=FC//128*D
+    plan=big_plan(dp,R); n=len(plan[0][0])
+    full=pl.BlockSpec((T,D),lambda c:(0,0))
+    m=lambda c: jnp.minimum(c,CH-1)
+    fin=R>>n
+    recv=[pltpu.VMEM((CH,rows>>(s+1),128),BF) for _,_,rows in plan for s in range(n)]
+    return pl.pallas_call(functools.partial(ffn_kernel,dp),grid=(CH+LAG*n+1,),
+      in_specs=[full]*4+[pl.BlockSpec((D,FC),lambda c:(0,m(c))),pl.BlockSpec((FC,D),lambda c:(m(c),0)),pl.BlockSpec((1,FC),lambda c:(0,m(c)))],
+      out_specs=[full,full,pl.BlockSpec((1,FC),lambda c:(0,m(c))),pl.BlockSpec((CH,fin,128),lambda c:(0,0,0))],
+      out_shape=[jax.ShapeDtypeStruct((T,D),F32)]*2+[jax.ShapeDtypeStruct((1,FF),F32),jax.ShapeDtypeStruct((CH,fin,128),BF)],
+      scratch_shapes=[pltpu.VMEM((T,FC),BF)]*2+[pltpu.VMEM((CH,2,R,128),BF),pltpu.VMEM((CH,R,128),BF)]+recv
+        +[pltpu.SemaphoreType.DMA((len(plan),n,CH))]*2+[pltpu.SemaphoreType.DMA((CH,))]*2,
+      compiler_params=pltpu.CompilerParams(vmem_limit_bytes=60*2**20,collective_id=0,has_side_effects=True),name="feed_forward")(n2,n2T,cot,cotT,wu,wd,bu)
+
+def finish_kernel(dp,red,heads,vec,up,down,heads_out,vec_out,full,hp,hg,vbuf,vrecv,*rest):
+    CH=full.shape[0]; R=full.shape[2]; D=up.shape[0]
+    plan=big_plan(dp,R); n=len(plan[0][0]); K=len(plan)
+    HR=hp.shape[2]; hplan=head_plan(dp,HR); HK=len(hplan)
+    hrecv=[rest[k*n:(k+1)*n] for k in range(HK)]
+    send_sem,recv_sem,chip_send,chip_got,hs_sem,hr_sem,ha_send,ha_recv,vs_sem,vr_sem=rest[HK*n:]
+    p=Peers(); g=pl.program_id(0); last=pl.num_programs(0)-1
+    regs=[halves(p,*s) for s in plan]
+    hregs=[halves(p,*s,keep_tw=True) for s in hplan]
+    def gat(k,s,c,landed):
+        other,mine,nr=regs[k][s]
+        ref=full.at[c,p.th,rows_at(other if landed else mine,nr),:]
+        return send(ref,ref,send_sem.at[k,s,c],recv_sem.at[k,s,c],p.peer(plan[k][0][s]))
+    def chip(c,landed):
+        ref=full.at[c,1-p.th if landed else p.th]
+        return send(ref,ref,chip_send.at[c],chip_got.at[c],p.peer("th"))
+    def hsum(k,s,c):
+        order=hplan[k][0]; other,_,nr=hregs[k][s]
+        if order[s]=="tw": src=hp.at[c,pl.ds(1,1),rows_at(other,nr),:]
+        elif order.index("tw")>s: src=hp.at[c,:,rows_at(other,nr),:]
+        else: src=hp.at[c,pl.ds(0,1),rows_at(other,nr),:]
+        return send(src,hrecv[k][s].at[c],hs_sem.at[k,s,c],hr_sem.at[k,s,c],p.peer(order[s]))
+    def hgat(k,s,c,landed):
+        order=hplan[k][0]; other,mine,nr=hregs[k][s]
+        ref=hg.at[c,rows_at(other if landed else mine,nr),:]
+        return send(ref,ref,ha_send.at[k,s,c],ha_recv.at[k,s,c],p.peer(order[s]))
+    backs=[[s for s in reversed(range(n)) if o[s]!="tw"] for o,_,_ in hplan]
+    vaxes=["th","tw"]+list(range(n-1))
+    def vcopy(i): return send(vbuf.at[i],vrecv.at[i],vs_sem.at[i],vr_sem.at[i],p.peer(vaxes[i]))
+    @pl.when(g==0)
+    def _():
+        out=0
+        for k in range(K):
+            _,kr,nr=regs[k][n-1]
+            for c in range(CH): full[c,p.th,rows_at(kr,nr),:]=red[c,out:out+nr,:]
+            out+=nr
+        for c in range(hp.shape[0]):
+            hp[c]=heads[:,c*HR:(c+1)*HR,:]
+        vbuf[0]=vec[...]
+        barrier(p,["th"]+plan[0][0])
+    steps=n+n-1
+    for j in range(steps+1):
+        for c in range(hp.shape[0]):
+            @pl.when(g==HSP*c+HLAG*j)
+            def _():
+                for k in range(HK):
+                    order=hplan[k][0]
+                    if 0<j<=n:
+                        s=j-1
+                        hsum(k,s,c).wait_recv()
+                        _,kr,nr=hregs[k][s]
+                        q=slice(0,2) if order.index("tw")>s else slice(0,1)
+                        at=(c,q,rows_at(kr,nr),slice(None))
+                        new=(hp[at].astype(F32)+hrecv[k][s][c].astype(F32)).astype(BF)
+                        if j<n: hp[at]=new
+                        else: hg[c,rows_at(kr,nr),:]=new[0]
+                    elif j>n: hgat(k,backs[k][j-n-1],c,True).wait_recv()
+                for k in range(HK):
+                    if j<n: hsum(k,j,c).start()
+                    elif j<steps: hgat(k,backs[k][j-n],c,False).start()
+                if j==steps: heads_out[c*HR:(c+1)*HR,:]=hg[c]
+    for i in range(len(vaxes)+1):
+        @pl.when(g==HLAG*i)
+        def _():
+            if i>0:
+                vcopy(i-1).wait_recv()
+                x=vbuf[i-1]+vrecv[i-1]
+                if i<len(vaxes): vbuf[i]=x
+                else: vec_out[...]=x
+            if i<len(vaxes): vcopy(i).start()
+    for j in reversed(range(n+1)):
+        c=g-GLAG*j
+        @pl.when((c>=0)&(c<CH))
+        def _():
+            if j>0:
+                for k in range(K): gat(k,n-j,c,True).wait_recv()
+            if j<n:
+                for k in range(K): gat(k,n-1-j,c,False).start()
+            else: chip(c,False).start()
+    c=g-GLAG*(n+1)
+    @pl.when((c>=0)&(c<CH))
+    def _():
+        chip(c,True).wait_recv()
+        for q in range(FC//128):
+            cols=slice(q*128,(q+1)*128)
+            up[:,cols]=full[c,0,q*D:(q+1)*D,:]
+            down[:,cols]=full[c,1,q*D:(q+1)*D,:]
+    @pl.when(g==last)
+    def _():
+        def drain(c,_):
+            chip(c,False).wait_send()
+            for k in range(K):
+                for s in range(n): gat(k,s,c,False).wait_send()
+            return 0
+        lax.fori_loop(0,CH,drain,0)
+        for c in range(hp.shape[0]):
+            for k in range(HK):
+                for s in range(n): hsum(k,s,c).wait_send()
+                for s in backs[k]: hgat(k,s,c,False).wait_send()
+        for i in range(len(vaxes)): vcopy(i).wait_send()
+
+def finish(dp,red,heads,vec,D):
+    CH,fin,_=red.shape; R=FC//128*D
+    plan=big_plan(dp,R); n=len(plan[0][0])
+    HRA=heads.shape[1]; HR=HRA//HC; hplan=head_plan(dp,HR)
+    m=lambda g: jnp.clip(g-GLAG*(n+1),0,CH-1)
+    hrecv=[]
+    for order,_,rows in hplan:
+        q=2
+        for axis in order:
+            if axis=="tw": q=1
+            else: rows//=2
+            hrecv.append(pltpu.VMEM((HC,q,rows,128),BF))
+    V=vec.shape[0]; nv=n+1
+    whole=lambda x: pl.BlockSpec(x.shape,lambda g:(0,)*x.ndim)
+    grid=max(CH+GLAG*(n+1),HSP*(HC-1)+HLAG*(2*n-1)+1,HLAG*nv+1)
+    return pl.pallas_call(functools.partial(finish_kernel,dp),grid=(grid,),
+      in_specs=[whole(red),whole(heads),whole(vec)],
+      out_specs=[pl.BlockSpec((D,FC),lambda g:(0,m(g)))]*2+[pl.BlockSpec((HRA,128),lambda g:(0,0)),whole(vec)],
+      out_shape=[jax.ShapeDtypeStruct((D,CH*FC),BF)]*2+[jax.ShapeDtypeStruct((HRA,128),BF),jax.ShapeDtypeStruct(vec.shape,F32)],
+      scratch_shapes=[pltpu.VMEM((CH,2,R,128),BF),pltpu.VMEM((HC,2,HR,128),BF),pltpu.VMEM((HC,HR,128),BF),pltpu.VMEM((nv,V,128),F32),pltpu.VMEM((nv,V,128),F32)]+hrecv
+        +[pltpu.SemaphoreType.DMA((len(plan),n,CH))]*2+[pltpu.SemaphoreType.DMA((CH,))]*2+[pltpu.SemaphoreType.DMA((len(hplan),n,HC))]*4+[pltpu.SemaphoreType.DMA((nv,))]*2,
+      compiler_params=pltpu.CompilerParams(vmem_limit_bytes=60*2**20,collective_id=1,has_side_effects=True),name="finish_gradients")(red,heads,vec)
+
+
 EPSILON = 1e-06
 
 
@@ -186,6 +458,7 @@
 
 
 def body(
+    dp_size,
     tokens,
     segment_ids,
     norm1_gain,
@@ -223,29 +496,21 @@
     middle = inputs + sum_halves(mm("le,ed->ld", attended, w_out_heads), th) + b_out
     normed_two, norm_two_back = jax.vjp(layer_norm, middle, norm2_gain, norm2_shift)
     second_low = normed_two.astype(BF)
-    hidden_pre = mm("ld,df->lf", second_low, w_up) + b_up
-    activated, gelu_back = jax.vjp(gelu_exact, hidden_pre)
-    active_low = activated.astype(BF)
-    grad_w_down = mm("lf,ld->fd", active_low, cot)
-    grad_active = mm("ld,fd->lf", cot, w_down)
-    grad_hidden = gelu_back(grad_active)[0].astype(BF)
-    grad_w_up = mm("ld,lf->df", second_low, grad_hidden)
-    big = lax.psum((grad_w_up.astype(BF), grad_w_down.astype(BF)), ("dp", "th", "tw"))
-    block_out = middle + (mm("lf,fd->ld", active_low, w_down) + b_down)
+    ffn_out, grad_normed_two, grad_b_up, red = ffn(
+        dp_size, second_low, second_low.T, cot, cot.T, w_up, w_down, b_up[None]
+    )
+    block_out = middle + (ffn_out + b_down)
     block_out = back_rows(block_out.astype(BF), tw)
     upstream = cot.astype(F32)
     grad_b_down = jnp.sum(upstream, axis=0)
-    grad_b_up = jnp.sum(grad_hidden.astype(F32), axis=0)
-    grad_normed_two = mm("lf,df->ld", grad_hidden, w_up)
     grad_mid_norm, grad_gain_two, grad_shift_two = norm_two_back(grad_normed_two)
     grad_middle = upstream + grad_mid_norm
     grad_branch = grad_middle.astype(BF)
     grad_b_out = jnp.sum(grad_branch.astype(F32), axis=0)
     grad_whole = whole_row(grad_branch, th)
     grad_heads = mm("ld,ed->le", grad_whole, w_out_heads).astype(BF)
-    grad_w_out = mm("le,ld->ed", attended, grad_whole)
+    grad_w_out = mm("ld,le->de", grad_whole, attended).astype(BF)
     dq, dk, dv = attn_bwd(query, key, value, grad_heads, attended, totals, *tables)
-    grad_w_qkv = jnp.stack([mm("ld,le->de", normed_row, g) for g in (dq, dk, dv)])
     grad_normed = (
         mm("le,de->ld", dq, w_heads[0]) + mm("le,de->ld", dk, w_heads[1]) + mm("le,de->ld", dv, w_heads[2])
     )
@@ -253,40 +518,42 @@
     grad_inputs, grad_gain_one, grad_shift_one = norm_one_back(grad_tile)
     grad_tokens = back_rows((grad_middle + grad_inputs).astype(BF), tw)
 
-    def reduce_heads(grad, axis):
-        own = lax.slice_in_dim(grad, 0, mine, axis=axis)
-        other = lax.slice_in_dim(grad, mine, 2 * mine, axis=axis)
-        return (own + swap(other.astype(BF), "tw").astype(F32)).astype(BF)
-
-    heads = lax.psum((reduce_heads(grad_w_qkv, 2), reduce_heads(grad_w_out, 0)), "dp")
+    grad_w = [mm("ld,le->de", normed_row, g).astype(BF) for g in (dq, dk, dv)] + [grad_w_out]
+    heads = jnp.stack(
+        [jnp.concatenate([g[:, q * mine : (q + 1) * mine] for g in grad_w], 1) for q in range(2)]
+    )
+    heads = heads.reshape(2, d, -1, 128).transpose(0, 2, 1, 3).reshape(2, -1, 128)
     grad_b = jnp.stack([jnp.sum(dq.astype(F32), 0), jnp.sum(dv.astype(F32), 0)])
     place = jnp.zeros((2, d), F32)
     place = lax.dynamic_update_slice(place, grad_b[:, :mine], (0, (2 * th + tw) * mine))
     place = lax.dynamic_update_slice(place, grad_b[:, mine:], (0, (2 * th + 1 - tw) * mine))
     vectors = (grad_gain_one, grad_shift_one, grad_b_out, grad_gain_two, grad_shift_two, grad_b_down, grad_b_up, place.reshape(-1))
-    small = lax.psum(jnp.concatenate(vectors), ("dp", "th", "tw"))
+    small = jnp.concatenate([v.reshape(-1) for v in vectors]).reshape(-1, 128)
+    up, down, heads, small = finish(dp_size, red, heads, small, d)
+    small = small.reshape(-1)
+    heads = heads.reshape(-1, d, 128).transpose(1, 0, 2).reshape(d, 4, mine).astype(F32)
     small_b_qv = lax.dynamic_slice_in_dim(small[-2 * d :].reshape(2, d), (2 * th + tw) * mine, mine, 1)
     return (
         block_out,
         grad_tokens,
         small[:d],
         small[d : 2 * d],
-        heads[0].astype(F32),
+        heads[:, :3].transpose(1, 0, 2),
         small_b_qv,
-        heads[1].astype(F32),
+        heads[:, 3].T,
         small[2 * d : 3 * d],
         small[3 * d : 4 * d],
         small[4 * d : 5 * d],
-        big[0].astype(F32),
+        up.astype(F32),
         small[6 * d : -2 * d],
-        big[1].astype(F32),
+        down.astype(F32).T,
         small[5 * d : 6 * d],
     )
 
 
 def solution(mesh):
     return jax.shard_map(
-        body,
+        functools.partial(body, mesh.shape["dp"]),
         mesh=mesh,
         in_specs=(
             P("dp", ("th", "tw"), None),

time: 553 us -> 438 us (0.79)
  waiting for transfers between devices: 226 us -> 52.6 us
  Pallas kernels: 62.9 us -> 209 us
  matrix products: 112 us -> 43.4 us
  blocking collectives: 48.9 us -> 0 us
  local copies, waits for them, and re-layouts: 20.8 us -> 58.3 us
  between operations: 15.4 us -> 1.65 us
  other arithmetic: 49.6 us -> 55.6 us
    psum x2 -> x0, waiting for transfers between devices: 188 us -> none  [the longest x1 188 us: body(): lax.psum((grad_w_up.astype(BF), grad_w_down.astype(BF)), ('dp', 'th', 'tw'))]
    pallas_call x0 -> x2, Pallas kernels: none -> 147 us  [the longest x1 80.8 us: finish(): pl.pallas_call(functools.partial(finish_kernel, dp), grid=(grid,), in_spe...]
    dot_general x18 -> x12, matrix products: 112 us -> 43.4 us  [mm(): return jnp.einsum(spec, a, b, preferred_element_type=F32)]
    psum x1 -> x0, blocking collectives: 48.9 us -> none  [body(): small = lax.psum(jnp.concatenate(vectors), ('dp', 'th', 'tw'))]
    ppermute x13 -> x11, waiting for transfers between devices: 37.7 us -> 52.6 us  [swap(): return lax.ppermute(value, axis, SWAP)]
    unnamed x123 -> x102, local copies, waits for them, and re-layouts: 10.1 us -> 22.3 us
    transpose x0 -> x2, other arithmetic: none -> 8.68 us  [the longest x1 7.27 us: body(): down.astype(F32)]
    pallas_call x0 -> x2, local copies, waits for them, and re-layouts: none -> 6.59 us  [ffn(): pl.pallas_call(functools.partial(ffn_kernel, dp), grid=(CH + LAG * n + 1,...]
  transfers between devices with their start and end apart: 15 -> 11, of which waited for: 4 -> 4; matrix products, arithmetic and copies ran while one was open for 21% -> 15% of each run, Pallas kernels for 6% -> 0%
where the time goes in v2:
time: 438 us; the launch traced here: 431 us
  Pallas kernels  209 us (48%)
  local copies, waits for them, and re-layouts  58.3 us (13%)
  other arithmetic  55.6 us (13%)
  waiting for transfers between devices  52.6 us (12%)
  matrix products  43.4 us (10%)
  starting transfers between devices  9.86 us (2%)
    pallas_call x1, Pallas kernels, finish(): pl.pallas_call(functools.partial(finish_kernel, dp), grid=(grid,), in_spe...  80.8 us
    pallas_call x1, Pallas kernels, ffn(): pl.pallas_call(functools.partial(ffn_kernel, dp), grid=(CH + LAG * n + 1,...  65.9 us
    ppermute x11, waiting for transfers between devices, swap(): return lax.ppermute(value, axis, SWAP)  52.6 us
    dot_general x12, matrix products, mm(): return jnp.einsum(spec, a, b, preferred_element_type=F32)  43.4 us
    pallas_call x1, Pallas kernels, attn_bwd(): pl.pallas_call(bwd_kernel, grid_spec=pltpu.PrefetchScalarGridSpec(num_sca...  35.1 us
    pallas_call x1, Pallas kernels, attn_fwd(): pl.pallas_call(fwd_kernel, grid_spec=pltpu.PrefetchScalarGridSpec(num_sca...  27.5 us
    unnamed x102, local copies, waits for them, and re-layouts  22.3 us
    ppermute x11, starting transfers between devices, swap(): return lax.ppermute(value, axis, SWAP)  9.86 us
  transfers between devices with their start and end apart: 11, of which 4 were waited for; matrix products, arithmetic and copies ran while one was open for 15% of the time, Pallas kernels for 0%

profile of v2, /device:TPU:0, one launch (start us, length us, event | category | flops | bytes accessed | tf_op | source)
XLA Modules:
  0.0 430.7 jit_solution(18284392137865870729)
XLA Ops:
  2.3 3.0 collective-permute-start
  8.8 10.7 %collective-permute-done = bf16[384,768]{0,1:T(8,128)(2,1)S(1)} collective-permute-done((bf16[384,768]{0,1:T(8,128)(2,1)S(1)}, bf16[384,768]{0,1:T(8,128)(2,1)S(1)}, u32[]{:S(2)}, u32[]{:S(2)}) %collective-permute-start) | collective-permute-done | bytes 589856 | tf_op jit(solution)/shard_map/ppermute | solution.py:422
  28.0 16.1 %collective-permute-done.2 = bf16[3,768,192]{1,2,0:T(8,128)(2,1)} collective-permute-done((bf16[3,768,192]{1,2,0:T(8,128)(2,1)}, bf16[3,768,192]{1,2,0:T(8,128)(2,1)}, u32[]{:S(2)}, u32[]{:S(2)}) %collective-permute-start.2) | collective-permute-done | bytes 884768 | tf_op jit(solution)/shard_map/ppermute | solution.py:422
  45.4 5.4 %convolution_convert_fusion.1.k_ref = bf16[1536,384]{1,0:T(8,128)(2,1)} fusion(bf16[3,768,384]{1,2,0:T(8,128)(2,1)S(1)} %constant_dynamic-update-slice_fusion, bf16[768,768]{0,1:T(8,128)(2,1)} %collective-permute-done.1, bf16[768,768]{0,1:T(8,128)(2,1)} %fusion.10, pred[]{:T(512)S(6)} %eq.11), kind=kOutput, calls=%fused_computation.18 | convolution fusion | flops 917176320 | bytes 4128769 | tf_op jit(solution)/shard_map/ld,de->le/dot_general | solution.py:457
  50.8 5.0 %fusion.5.v_ref = bf16[1536,384]{1,0:T(8,128)(2,1)} fusion(f32[384]{0:T(512)S(1)} %get-tuple-element.76, bf16[3,768,384]{1,2,0:T(8,128)(2,1)S(1)} %constant_dynamic-update-slice_fusion, bf16[768,768]{0,1:T(8,128)(2,1)} %collective-permute-done.1, bf16[768,768]{0,1:T(8,128)(2,1)} %fusion.10, pred[]{:T(512)S(6)} %eq.11), kind=kOutput, calls=%fused_computation.16 | convolution fusion | flops 917766144 | bytes 4130817 | tf_op jit(solution)/shard_map/ld,de->le/dot_general | solution.py:457
  55.8 5.0 %fusion.8.q_ref = bf16[1536,384]{1,0:T(8,128)(2,1)} fusion(f32[384]{0:T(512)S(1)} %get-tuple-element.77, bf16[3,768,384]{1,2,0:T(8,128)(2,1)S(1)} %constant_dynamic-update-slice_fusion, bf16[768,768]{0,1:T(8,128)(2,1)} %collective-permute-done.1, bf16[768,768]{0,1:T(8,128)(2,1)} %fusion.10, pred[]{:T(512)S(6)} %eq.11), kind=kOutput, calls=%fused_computation.21 | convolution fusion | flops 918355968 | bytes 4130817 | tf_op jit(solution)/shard_map/ld,de->le/dot_general | solution.py:457
  60.8 27.5 %attention_forward.1 = (bf16[1536,384]{1,0:T(8,128)(2,1)}, f32[8,1536]{1,0:T(8,128)}) custom-call(s32[6]{0:T(128)} %get-tuple-element.113.lo_ref, s32[6]{0:T(128)} %get-tuple-element.112.hi_ref, bf16[1536,384]{1,0:T(8,128)(2,1)} %fusion.8.q_ref, bf16[1536,384]{1,0:T(8,128)(2,1)} %convolution_convert_fusion.1.k_ref, bf16[1536,384]{1,0:T(8,128)(2,1)} %fusion.5.v_ref, ...), custom_call_target="tpu_custom_call" | custom-call | tf_op jit(solution)/shard_map/attention_forward/pallas_call | solution.py:57
  96.0 12.5 %collective-permute-done.6 = bf16[384,768]{0,1:T(8,128)(2,1)S(1)} collective-permute-done((bf16[384,768]{0,1:T(8,128)(2,1)S(1)}, bf16[384,768]{0,1:T(8,128)(2,1)S(1)}, u32[]{:S(2)}, u32[]{:S(2)}) %collective-permute-start.6) | collective-permute-done | bytes 589856 | tf_op jit(solution)/shard_map/ppermute | solution.py:422
  121.8 65.9 %feed_forward.1 = (f32[768,768]{1,0:T(8,128)}, f32[768,768]{1,0:T(8,128)}, f32[1,3072]{1,0:T(1,128)}, bf16[6,192,128]{2,1,0:T(8,128)(2,1)}) custom-call(bf16[768,768]{1,0:T(8,128)(2,1)} %copy.55.n2, bf16[768,768]{1,0:T(8,128)(2,1)} %fusion.50.n2T, bf16[768,768]{1,0:T(8,128)(2,1)} %copy.56.cot, bf16[768,768]{1,0:T(8,128)(2,1)} %bitcast.79, ...), custom_call_target="tpu_custom_call" | custom-call | tf_op jit(solution)/shard_map/feed_forward/pallas_call | solution.py:271
  187.7 3.0 copy.57
  190.7 3.5 copy.58
  194.4 3.2 multiply_reduce_fusion
  207.0 13.4 %collective-permute-done.7 = bf16[384,768]{0,1:T(8,128)(2,1)} collective-permute-done((bf16[384,768]{0,1:T(8,128)(2,1)}, bf16[384,768]{0,1:T(8,128)(2,1)}, u32[]{:S(2)}, u32[]{:S(2)}) %collective-permute-start.7) | collective-permute-done | bytes 589856 | tf_op jit(solution)/shard_map/ppermute | solution.py:422
  223.7 4.8 %convolution_convert_fusion.do_ref = bf16[1536,384]{1,0:T(8,128)(2,1)} fusion(bf16[384,768]{1,0:T(8,128)(2,1)S(1)} %copy-done.20, bf16[768,768]{0,1:T(8,128)(2,1)} %collective-permute-done.8, bf16[768,768]{0,1:T(8,128)(2,1)} %get-tuple-element.81, pred[]{:T(512)S(6)} %eq.11), kind=kOutput, calls=%fused_computation.17 | convolution fusion | flops 917176320 | bytes 4128769 | tf_op jit(solution)/shard_map/ld,ed->le/dot_general | solution.py:457
  228.6 35.1 %attention_backward.1 = (bf16[1536,384]{1,0:T(8,128)(2,1)}, bf16[1536,384]{1,0:T(8,128)(2,1)}, bf16[1536,384]{1,0:T(8,128)(2,1)}) custom-call(s32[6]{0:T(128)} %get-tuple-element.113.lo_ref, s32[6]{0:T(128)} %get-tuple-element.112.hi_ref, bf16[1536,384]{1,0:T(8,128)(2,1)} %fusion.8.q_ref, bf16[1536,384]{1,0:T(8,128)(2,1)} %convolution_convert_fusion.1.k_ref, ...), custom_call_target="tpu_custom_call" | custom-call | tf_op jit(solution)/shard_map/attention_backward/pallas_call | solution.py:114
  268.0 3.7 convolution_convert_fusion.2
  274.7 3.7 convolution_convert_fusion.4
  279.2 3.7 convolution_convert_fusion.3
  289.6 3.7 convolution_convert_fusion.5
  307.3 80.8 %finish_gradients.1 = (bf16[768,3072]{1,0:T(8,128)(2,1)}, bf16[768,3072]{1,0:T(8,128)(2,1)}, bf16[4608,128]{1,0:T(8,128)(2,1)}, f32[72,128]{1,0:T(8,128)}) custom-call(bf16[6,192,128]{2,1,0:T(8,128)(2,1)} %get-tuple-element.34.red, bf16[2,4608,128]{2,1,0:T(8,128)(2,1)} %bitcast.80, f32[72,128]{1,0:T(8,128)} %bitcast.89), custom_call_target="tpu_custom_call" | custom-call | tf_op jit(solution)/shard_map/finish_gradients/pallas_call | solution.py:395
  391.6 3.2 add_convert_fusion
  398.4 7.3 %convert_bitcast_fusion = f32[3072,768]{0,1:T(8,128)} fusion(bf16[768,3072]{1,0:T(8,128)(2,1)} %get-tuple-element.39), kind=kLoop, calls=%fused_computation | loop fusion | flops 2359296 | bytes 14155776 | tf_op jit(solution)/shard_map/transpose | solution.py:549
  408.3 7.4 %convert_element_type.124 = f32[768,3072]{1,0:T(8,128)} convert(bf16[768,3072]{1,0:T(8,128)(2,1)} %get-tuple-element.38) | non-fusion elementwise | flops 2359296 | bytes 14155776 | tf_op jit(solution)/shard_map/convert_element_type | solution.py:547
  415.7 9.6 %copy.68 = f32[3072,768]{1,0:T(8,128)} copy(f32[3072,768]{0,1:T(8,128)} %convert_bitcast_fusion) | data formatting | bytes 18874368
  (197 shorter events, 91.8 us)
Async XLA Ops:
  0.6 7.1 %copy-start = (s32[2,1536]{1,0:T(2,128)S(1)}, s32[2,1536]{1,0:T(2,128)}, u32[]{:S(2)}) copy-start(s32[2,1536]{1,0:T(2,128)} %param.16) | copy-start | bytes 36868
  2.0 18.4 %copy-start.24 = (f32[768]{0:T(1024)S(1)}, f32[768]{0:T(1024)}, u32[]{:S(2)}) copy-start(f32[768]{0:T(1024)} %param.17) | copy-start | bytes 9220
  2.0 18.4 %copy-start.42 = (f32[768]{0:T(1024)S(1)}, f32[768]{0:T(1024)}, u32[]{:S(2)}) copy-start(f32[768]{0:T(1024)} %param.18) | copy-start | bytes 9220
  2.3 17.2 %collective-permute-start = (bf16[384,768]{0,1:T(8,128)(2,1)S(1)}, bf16[384,768]{0,1:T(8,128)(2,1)S(1)}, u32[]{:S(2)}, u32[]{:S(2)}) collective-permute-start(bf16[384,768]{0,1:T(8,128)(2,1)S(1)} %bitcast.87), channel_id=1, source_target_pairs={{0,1},{1,0},{2,3},{3,2},{4,5},{5,4},{6,7},{7,6},{8,9},{9,8},{10,11... | collective-permute-start | bytes 1769480 | tf_op jit(solution)/shard_map/ppermute | solution.py:422
  5.4 20.8 %collective-permute-start.3 = (f32[2,192]{1,0:T(2,128)}, f32[2,192]{1,0:T(2,128)}, u32[]{:S(2)}, u32[]{:S(2)}) collective-permute-start(f32[2,192]{1,0:T(2,128)} %param.20), channel_id=1, source_target_pairs={{0,1},{1,0},{2,3},{3,2},{4,5},{5,4},{6,7},{7,6},{8,9},{9,8},{10,11... | collective-permute-start | bytes 4616 | tf_op jit(solution)/shard_map/ppermute | solution.py:422
  5.4 21.6 %collective-permute-start.4 = (bf16[192,768]{1,0:T(8,128)(2,1)}, bf16[192,768]{1,0:T(8,128)(2,1)}, u32[]{:S(2)}, u32[]{:S(2)}) collective-permute-start(bf16[192,768]{1,0:T(8,128)(2,1)} %param.21), channel_id=1, source_target_pairs={{0,1},{1,0},{2,3},{3,2},{4,5},{5,4},{6,7},{7,6},{8,9},{9,8},{10,11... | collective-permute-start | bytes 884744 | tf_op jit(solution)/shard_map/ppermute | solution.py:422
  7.4 36.7 %collective-permute-start.2 = (bf16[3,768,192]{1,2,0:T(8,128)(2,1)}, bf16[3,768,192]{1,2,0:T(8,128)(2,1)}, u32[]{:S(2)}, u32[]{:S(2)}) collective-permute-start(bf16[3,768,192]{1,2,0:T(8,128)(2,1)} %param.19), channel_id=1, source_target_pairs={{0,1},{1,0},{2,3},{3,2},{4,5},{5,4},{6,7},{7,6},{8,9},{9,8},{10,11... | collective-permute-start | bytes 2654216 | tf_op jit(solution)/shard_map/ppermute | solution.py:422
  20.4 5.8 %copy-start.29 = (f32[768]{0:T(1024)}, f32[768]{0:T(1024)S(1)}, u32[]{:S(2)}) copy-start(f32[768]{0:T(1024)S(1)} %fusion.12) | copy-start | bytes 9220
  20.4 5.8 %copy-start.25 = (f32[768]{0:T(1024)}, f32[768]{0:T(1024)S(1)}, u32[]{:S(2)}) copy-start(f32[768]{0:T(1024)S(1)} %fusion.22) | copy-start | bytes 9220
  22.0 23.4 %collective-permute-start.1 = (bf16[768,768]{0,1:T(8,128)(2,1)}, bf16[768,768]{0,1:T(8,128)(2,1)}, u32[]{:S(2)}, u32[]{:S(2)}) collective-permute-start(bf16[768,768]{0,1:T(8,128)(2,1)} %fusion.10), channel_id=1, source_target_pairs={{0,2},{2,0},{1,3},{3,1},{4,6},{6,4},{5,7},{7,5},{8,10},{10,8},{9,1... | collective-permute-start | bytes 3538952 | tf_op jit(solution)/shard_map/ppermute | solution.py:422
  28.0 60.3 %copy-start.19 = (bf16[384,768]{1,0:T(8,128)(2,1)}, bf16[384,768]{1,0:T(8,128)(2,1)S(1)}, u32[]{:S(2)}) copy-start(bf16[384,768]{1,0:T(8,128)(2,1)S(1)} %constant_dynamic-update-slice_fusion.2) | copy-start | bytes 1769476
  45.3 10.4 %copy-start.15 = (bf16[3,768,384]{1,2,0:T(8,128)(2,1)}, bf16[3,768,384]{1,2,0:T(8,128)(2,1)S(1)}, u32[]{:S(2)}) copy-start(bf16[3,768,384]{1,2,0:T(8,128)(2,1)S(1)} %constant_dynamic-update-slice_fusion) | copy-start | bytes 5308420
  92.3 20.8 %collective-permute-start.5 = (bf16[768,768]{0,1:T(8,128)(2,1)}, bf16[768,768]{0,1:T(8,128)(2,1)}, u32[]{:S(2)}, u32[]{:S(2)}) collective-permute-start(bf16[768,768]{0,1:T(8,128)(2,1)} %dynamic-slice_convert_fusion.1), channel_id=1, source_target_pairs={{0,2},{2,0},{1,3},{3,1},{4,6},{6,4},{5,7},{7,5},{8,10},{10,8},{9,1... | collective-permute-start | bytes 3538952 | tf_op jit(solution)/shard_map/ppermute | solution.py:422
  93.9 14.6 %collective-permute-start.6 = (bf16[384,768]{0,1:T(8,128)(2,1)S(1)}, bf16[384,768]{0,1:T(8,128)(2,1)S(1)}, u32[]{:S(2)}, u32[]{:S(2)}) collective-permute-start(bf16[384,768]{0,1:T(8,128)(2,1)S(1)} %bitcast.88), channel_id=1, source_target_pairs={{0,1},{1,0},{2,3},{3,2},{4,5},{5,4},{6,7},{7,6},{8,9},{9,8},{10,11... | collective-permute-start | bytes 1769480 | tf_op jit(solution)/shard_map/ppermute | solution.py:422
  109.3 3.7 copy-start.43
  201.7 4.5 %copy-start.10 = (f32[768,768]{1,0:T(8,128)S(1)}, f32[768,768]{1,0:T(8,128)}, u32[]{:S(2)}) copy-start(f32[768,768]{1,0:T(8,128)} %get-tuple-element.29) | copy-start | bytes 7077892
  201.7 22.0 %collective-permute-start.8 = (bf16[768,768]{0,1:T(8,128)(2,1)}, bf16[768,768]{0,1:T(8,128)(2,1)}, u32[]{:S(2)}, u32[]{:S(2)}) collective-permute-start(bf16[768,768]{0,1:T(8,128)(2,1)} %get-tuple-element.81), channel_id=1, source_target_pairs={{0,2},{2,0},{1,3},{3,1},{4,6},{6,4},{5,7},{7,5},{8,10},{10,8},{9,1... | collective-permute-start | bytes 3538952 | tf_op jit(solution)/shard_map/ppermute | solution.py:422
  204.2 16.2 %collective-permute-start.7 = (bf16[384,768]{0,1:T(8,128)(2,1)}, bf16[384,768]{0,1:T(8,128)(2,1)}, u32[]{:S(2)}, u32[]{:S(2)}) collective-permute-start(bf16[384,768]{0,1:T(8,128)(2,1)} %get-tuple-element.91), channel_id=1, source_target_pairs={{0,1},{1,0},{2,3},{3,2},{4,5},{5,4},{6,7},{7,6},{8,9},{9,8},{10,11... | collective-permute-start | bytes 1769480 | tf_op jit(solution)/shard_map/ppermute | solution.py:422
  268.0 4.5 %copy-start.14 = (bf16[1536,384]{1,0:T(8,128)(2,1)S(1)}, bf16[1536,384]{1,0:T(8,128)(2,1)}, u32[]{:S(2)}) copy-start(bf16[1536,384]{1,0:T(8,128)(2,1)} %get-tuple-element.33) | copy-start | bytes 3538948
  268.0 4.7 %copy-start.17 = (bf16[1536,384]{1,0:T(8,128)(2,1)S(1)}, bf16[1536,384]{1,0:T(8,128)(2,1)}, u32[]{:S(2)}) copy-start(bf16[1536,384]{1,0:T(8,128)(2,1)} %get-tuple-element.32) | copy-start | bytes 3538948
  288.5 12.2 %collective-permute-start.9 = (bf16[768,768]{0,1:T(8,128)(2,1)}, bf16[768,768]{0,1:T(8,128)(2,1)}, u32[]{:S(2)}, u32[]{:S(2)}) collective-permute-start(bf16[768,768]{0,1:T(8,128)(2,1)} %dynamic-slice_convert_fusion), channel_id=1, source_target_pairs={{0,2},{2,0},{1,3},{3,1},{4,6},{6,4},{5,7},{7,5},{8,10},{10,8},{9,1... | collective-permute-start | bytes 3538952 | tf_op jit(solution)/shard_map/ppermute | solution.py:422
  300.7 4.3 %copy-start.26 = (f32[768]{0:T(1024)S(1)}, f32[768]{0:T(1024)}, u32[]{:S(2)}) copy-start(f32[768]{0:T(1024)} %copy-done.25) | copy-start | bytes 9220
  305.0 86.6 %copy-start.4 = (bf16[768,768]{0,1:T(8,128)(2,1)S(1)}, bf16[768,768]{0,1:T(8,128)(2,1)}, u32[]{:S(2)}) copy-start(bf16[768,768]{0,1:T(8,128)(2,1)} %copy-done.2) | copy-start | bytes 3538948
  395.9 31.6 %collective-permute-start.10 = (bf16[384,768]{0,1:T(8,128)(2,1)}, bf16[384,768]{0,1:T(8,128)(2,1)}, u32[]{:S(2)}, u32[]{:S(2)}) collective-permute-start(bf16[384,768]{0,1:T(8,128)(2,1)} %get-tuple-element.89), channel_id=1, source_target_pairs={{0,1},{1,0},{2,3},{3,2},{4,5},{5,4},{6,7},{7,6},{8,9},{9,8},{10,11... | collective-permute-start | bytes 1769480 | tf_op jit(solution)/shard_map/ppermute | solution.py:422
  (32 other events, 74.3 us)
